TPU v7x, 256 devices: a whole 4x4x8 slice. The times are simulated.
256 devices in a mesh: mem: 32 (over y, z_lo, core), tile: 8 (over x, z_hi).
Axes of the slice: x: 4, y: 4, z: 8 (z_hi: 2, z_lo: 4; z = z_hi * 4 + z_lo), core: 2. Of those that a mesh axis runs over, the one named last changes fastest.
Arguments:
- weights: float32 [32, 8, 128, 512], P('mem', None, 'tile'), may hold values from -3 to 3
- perturb: bfloat16 [32, 8, 128, 512], P('mem', None, 'tile'), may hold values from -6 to 6
- coef_lon: float32 [8, 128, 512], P(None, 'tile'), may hold values from 0.01 to 0.09
- coef_lat: float32 [8, 128, 512], P(None, 'tile'), may hold values from 0.2 to 0.4
- obs_value: float32 [16384, 128], P(('mem', 'tile')), may hold values from -6 to 6
- obs_weight: float32 [16384, 128], P(('mem', 'tile')), may hold values from 0.25 to 4
- obs_segment: int32 [16384], P(('mem', 'tile')), may hold values from 0 to 511
- obs_kind: int32 [16384], P(('mem', 'tile')), may hold values from 0 to 3
- obs_target: int32 [16384, 1], P(('mem', 'tile')), may hold values from 0 to 7; in each aligned block of 64 rows (0 to 63, 64 to 127, ...) at most 16 rows name the same one
- obs_count: int32 [256], P(('mem', 'tile')), may hold values from 1 to 64, 8192 in all
- operators: float32 [4, 128, 128], replicated, may hold values from -0.5 to 0.5
Outputs:
- increment: float32 [8, 128, 512], P(None, 'tile')
- gradient: float32 [32, 8, 128, 512], P('mem', None, 'tile')
Inputs may be any that keep to these rules, and one draw needn't show every extreme that they name: `obs_target`: in the 64 rows of one owner no tile is named by more than 16 rows. The first obs_count slots of an owner hold observations, the others are empty and ignored.
All inputs are finite; a program needn't handle non-finite values. No bound on the sum of `obs_count` on one device may be relied on, other than what follows from the above.
Results may differ from a plain program's by a relative error of at most 0.0003.
Values sent between devices are 32-bit elements; how exact they have to be, the bound alone decides.
A program may use at most 64 MiB of HBM per device.

v0:
```python
import math

import jax
import jax.numpy as jnp
from jax import lax
from jax.sharding import PartitionSpec as P

SEG = 128
SWEEPS = 16


def extended_2(shard, sides, width):
    for axis, dim in sides:
        peers, length = (lax.axis_size(axis), shard.shape[dim])
        up = [(i, (i + 1) % peers) for i in range(peers - 1)]
        down = [(j, i) for i, j in up]
        last = lax.slice_in_dim(shard, length - width, length, axis=dim)
        first = lax.slice_in_dim(shard, 0, width, axis=dim)
        before = lax.ppermute(last, axis, up)
        after = lax.ppermute(first, axis, down)
        shard = jnp.concatenate([before, shard, after], axis=dim)
    return shard


def advance(current, padded, coef_lon, coef_lat):
    zonal_term = jnp.roll(current, 1, 2) + jnp.roll(current, -1, 2) - 2.0 * current
    across = padded[:, 2:] + padded[:, :-2] - 2.0 * current
    return current + coef_lon * zonal_term + coef_lat * across


def retreat(current, padded_lat, coef_lon, coef_lat):
    flux_lon = coef_lon * current
    retain = 1.0 - 2.0 * coef_lon - 2.0 * coef_lat
    return (
        retain * current
        + jnp.roll(flux_lon, 1, 2)
        + jnp.roll(flux_lon, -1, 2)
        + padded_lat[:, 2:]
        + padded_lat[:, :-2]
    )


def smooth_forward(current, coef_lon, coef_lat):
    for sweep_index in range(SWEEPS):
        padded = extended_2(current, (("tile", 1),), 1)
        current = advance(current, padded, coef_lon, coef_lat)
    return current


def smooth_adjoint(current, coef_lon, coef_lat):
    for sweep_index in range(SWEEPS):
        padded = extended_2(coef_lat * current, (("tile", 1),), 1)
        current = retreat(current, padded, coef_lon, coef_lat)
    return current


def observe(blocks, operators, kinds, values, precisions):
    images = jnp.einsum("bj,kij->kbi", blocks, operators, precision=lax.Precision.HIGHEST)
    choose = (kinds[None, :] == jnp.arange(operators.shape[0])[:, None]).astype(jnp.float32)[
        :, :, None
    ]
    modelled = jnp.sum(choose * images, 0)
    misfit = precisions * (modelled - values)
    return jnp.einsum(
        "kbi,kij->bj", choose * misfit[None], operators, precision=lax.Precision.HIGHEST
    )


def shards(
    weights,
    perturb,
    coef_lon,
    coef_lat,
    obs_value,
    obs_weight,
    obs_segment,
    obs_kind,
    obs_target,
    obs_count,
    operators,
):
    tiles = lax.axis_size("tile")
    scale = 1.0 / math.sqrt(lax.axis_size("mem"))
    member_weights = weights[0]
    member_perturb = perturb[0].astype(jnp.float32)
    product = member_perturb * smooth_forward(member_weights, coef_lon, coef_lat)
    summed = lax.psum(product, "mem")
    increment = summed * scale
    table = increment.reshape(-1, SEG)
    slots = obs_value.shape[0]
    capacity = 2 * slots // tiles
    live = jnp.arange(slots) < obs_count[0]
    target = obs_target[:, 0]
    onehot = (target[:, None] == jnp.arange(tiles)[None, :]).astype(jnp.int32)
    earlier = jnp.cumsum(onehot, 0) - onehot
    position = target * capacity + jnp.sum(earlier * onehot, 1)
    live_weight = obs_weight * live.astype(jnp.float32)[:, None]
    request = (
        jnp.full((tiles * capacity,), -1, jnp.int32)
        .at[position]
        .set(jnp.where(live, obs_segment, -1))
    )
    asked = lax.all_to_all(
        request.reshape(tiles, capacity), "tile", split_axis=0, concat_axis=0, tiled=True
    ).reshape(-1)
    valid = (asked >= 0).astype(jnp.float32)[:, None]
    index = jnp.maximum(asked, 0)
    found = table[index] * valid
    answered = lax.all_to_all(
        found.reshape(tiles, capacity, SEG), "tile", split_axis=0, concat_axis=0, tiled=True
    ).reshape(-1, SEG)
    adjoint = observe(answered[position], operators, obs_kind, obs_value, live_weight)
    outgoing = jnp.zeros((tiles * capacity, SEG), jnp.float32).at[position].set(adjoint)
    returned = lax.all_to_all(
        outgoing.reshape(tiles, capacity, SEG), "tile", split_axis=0, concat_axis=0, tiled=True
    ).reshape(-1, SEG)
    local_table = jnp.zeros_like(table).at[index].add(returned)
    adjoint_table = lax.psum(local_table, "mem")
    adjoint_field = adjoint_table.reshape(increment.shape)
    backward = smooth_adjoint(member_perturb * adjoint_field, coef_lon, coef_lat)
    member_gradient = member_weights + backward * scale
    return (increment, member_gradient[None])


def solution(mesh):
    placed = (
        P("mem", None, "tile", None),
        P("mem", None, "tile", None),
        P(None, "tile", None),
        P(None, "tile", None),
        P(("mem", "tile"), None),
        P(("mem", "tile"), None),
        P(("mem", "tile")),
        P(("mem", "tile")),
        P(("mem", "tile"), None),
        P(("mem", "tile")),
        P(),
    )
    return jax.shard_map(
        shards,
        mesh=mesh,
        in_specs=placed,
        out_specs=(P(None, "tile", None), P("mem", None, "tile", None)),
        check_vma=False,
    )
```

profile of v0, /device:TPU:6, one launch (start us, length us, event | category | flops | bytes accessed | tf_op | source)
XLA Modules:
  0.0 1062.2 jit_solution(6415799808595329105)
XLA Ops:
  12.3 11.4 %all-to-all-start = ((s32[8,1,16]{2,1,0:T(1,128)}), s32[8,1,16]{2,1,0:T(1,128)S(1)}, u32[]{:S(2)}, u32[]{:S(2)}) async-start(s32[8,1,16]{2,1,0:T(1,128)} %bitcast.7), calls=%async_computation | async-start | bytes 8192 | tf_op jit(solution)/shard_map/all_to_all | solution.py:103
  24.7 7.6 collective-permute-start
  36.2 6.5 collective-permute-done.1
  45.4 7.5 collective-permute-start.3
  53.0 2.9 collective-permute-done.3
  56.3 6.6 collective-permute-start.4
  62.9 3.2 collective-permute-start.5
  66.1 7.2 collective-permute-done.5
  76.0 7.5 collective-permute-start.7
  83.6 2.9 collective-permute-done.7
  86.8 6.6 collective-permute-start.8
  93.4 3.2 collective-permute-start.9
  96.7 7.2 collective-permute-done.9
  106.5 7.5 collective-permute-start.11
  114.1 2.8 collective-permute-done.11
  119.2 7.8 collective-permute-start.13
  127.2 2.5 collective-permute-done.13
  132.0 7.8 collective-permute-start.15
  139.9 2.7 collective-permute-done.15
  144.9 7.8 collective-permute-start.17
  152.8 2.5 collective-permute-done.17
  157.8 7.7 collective-permute-start.19
  165.6 2.6 collective-permute-done.19
  170.6 7.8 collective-permute-start.21
  178.5 2.5 collective-permute-done.21
  183.3 7.8 collective-permute-start.23
  191.2 2.5 collective-permute-done.23
  196.1 7.8 collective-permute-start.25
  204.0 2.5 collective-permute-done.25
  208.9 7.8 collective-permute-start.27
  216.8 2.5 collective-permute-done.27
  221.6 7.8 collective-permute-start.29
  229.5 2.5 collective-permute-done.29
  234.4 8.0 collective-permute-start.31
  242.5 2.5 collective-permute-done.31
  246.0 278.6 %all-reduce.3.cloned.1.call-done = f32[8,16,512]{2,1,0:T(8,128)} async-done(((f32[8,16,512]{2,1,0:T(8,128)}), f32[8,16,512]{2,1,0:T(8,128)}) %all-reduce.3.cloned.1.call-update) | async-done | bytes 262160 | tf_op jit(solution)/shard_map/psum | solution.py:87
  527.6 9.8 all-to-all-start.1
  537.4 8.3 all-to-all-done.1
  548.2 12.6 %all_to_all.19 = f32[8,16,128]{2,1,0:T(8,128)S(1)} all-to-all(f32[8,16,128]{2,1,0:T(8,128)S(1)} %bitcast.56), channel_id=1, replica_groups=mesh['mem'=32,'tile'=8] {'tile'}, dimensions={0} | all-to-all | bytes 131072 | tf_op jit(solution)/shard_map/all_to_all | solution.py:114
  562.8 271.9 %all-reduce.5.cloned.1.call-done = f32[8,16,512]{2,1,0:T(8,128)} async-done(((f32[8,16,512]{2,1,0:T(8,128)}), f32[8,16,512]{2,1,0:T(8,128)}) %all-reduce.5.cloned.1.call-update) | async-done | bytes 262160 | tf_op jit(solution)/shard_map/psum | solution.py:118
  835.8 7.8 collective-permute-start.32
  845.8 8.3 collective-permute-done.33
  856.4 8.0 collective-permute-start.35
  867.1 6.9 collective-permute-start.36
  874.1 2.8 collective-permute-start.37
  877.1 7.4 collective-permute-done.37
  886.7 7.8 collective-permute-start.39
  897.5 6.8 collective-permute-start.40
  904.2 3.0 collective-permute-start.41
  907.5 7.2 collective-permute-done.41
  917.1 7.6 collective-permute-start.43
  925.0 2.6 collective-permute-done.43
  929.8 7.8 collective-permute-start.45
  937.8 2.4 collective-permute-done.45
  942.4 7.8 collective-permute-start.47
  955.4 7.6 collective-permute-start.49
  963.2 2.7 collective-permute-done.49
  968.0 7.8 collective-permute-start.51
  980.7 7.8 collective-permute-start.53
  993.4 7.8 collective-permute-start.55
  1006.0 7.8 collective-permute-start.57
  1018.7 7.8 collective-permute-start.59
  1031.3 7.8 collective-permute-start.61
  1044.0 7.8 collective-permute-start.63
  (264 shorter events, 111.4 us)
Async XLA Ops:
  12.3 23.8 %all-to-all-start = ((s32[8,1,16]{2,1,0:T(1,128)}), s32[8,1,16]{2,1,0:T(1,128)S(1)}, u32[]{:S(2)}, u32[]{:S(2)}) async-start(s32[8,1,16]{2,1,0:T(1,128)} %bitcast.7), calls=%async_computation | async-start | bytes 8192 | tf_op jit(solution)/shard_map/all_to_all | solution.py:103
  23.7 500.8 %all-reduce.3.cloned.1.call-start = ((), (), s32[]{:S(2)}) async-start(), calls=%async_computation.3 | async-start | bytes 524288 | tf_op jit(solution)/shard_map/psum | solution.py:87
  24.7 11.5 %collective-permute-start = (f32[8,1,512]{2,1,0:T(1,128)S(1)}, f32[8,1,512]{2,1,0:T(1,128)S(1)}, u32[]{:S(2)}, u32[]{:S(2)}) collective-permute-start(f32[8,1,512]{2,1,0:T(1,128)S(1)} %get-tuple-element.225), channel_id=1, source_target_pairs={{1,0},{2,1},{3,2},{4,3},{5,4},{6,5},{7,6},{9,8},{10,9},{11,10},{12... | collective-permute-start | bytes 49160 | tf_op jit(solution)/shard_map/ppermute | solution.py:20
  32.3 10.4 collective-permute-start.1
  43.2 9.8 collective-permute-start.2
  45.4 10.5 collective-permute-start.3
  56.3 9.8 collective-permute-start.4
  62.9 10.4 collective-permute-start.5
  73.7 9.8 collective-permute-start.6
  76.0 10.4 collective-permute-start.7
  86.8 9.8 collective-permute-start.8
  93.4 10.4 collective-permute-start.9
  104.2 9.8 collective-permute-start.10
  106.5 10.4 collective-permute-start.11
  117.3 9.8 collective-permute-start.12
  119.2 10.4 collective-permute-start.13
  130.1 9.8 collective-permute-start.14
  132.0 10.6 collective-permute-start.15
  143.0 9.8 collective-permute-start.16
  144.9 10.4 collective-permute-start.17
  157.8 10.4 collective-permute-start.19
  168.6 9.8 collective-permute-start.20
  170.6 10.4 collective-permute-start.21
  181.4 9.8 collective-permute-start.22
  183.3 10.4 collective-permute-start.23
  196.1 10.4 collective-permute-start.25
  208.9 10.4 collective-permute-start.27
  221.6 10.4 collective-permute-start.29
  232.5 10.0 collective-permute-start.30
  234.4 10.6 collective-permute-start.31
  527.6 18.1 %all-to-all-start.1 = ((f32[8,16,128]{2,1,0:T(8,128)}), f32[8,16,128]{2,1,0:T(8,128)S(1)}, u32[]{:S(2)}, u32[]{:S(2)}) async-start(f32[8,16,128]{2,1,0:T(8,128)} %broadcast_multiply_fusion.1), calls=%async_computation.1 | async-start | bytes 131072 | tf_op jit(solution)/shard_map/all_to_all | solution.py:109
  537.4 297.4 %all-reduce.5.cloned.1.call-start = ((), (), s32[]{:S(2)}) async-start(), calls=%async_computation.4 | async-start | bytes 524288 | tf_op jit(solution)/shard_map/psum | solution.py:118
  835.8 10.0 collective-permute-start.32
  843.6 10.5 collective-permute-start.33
  854.4 10.2 collective-permute-start.34
  856.4 10.5 collective-permute-start.35
  867.1 10.0 collective-permute-start.36
  874.1 10.4 collective-permute-start.37
  884.8 10.0 collective-permute-start.38
  886.7 10.4 collective-permute-start.39
  897.5 10.0 collective-permute-start.40
  904.2 10.4 collective-permute-start.41
  915.0 10.0 collective-permute-start.42
  917.1 10.4 collective-permute-start.43
  927.8 10.0 collective-permute-start.44
  929.8 10.4 collective-permute-start.45
  940.5 10.0 collective-permute-start.46
  942.4 10.4 collective-permute-start.47
  953.2 10.0 collective-permute-start.48
  955.4 10.4 collective-permute-start.49
  966.1 10.0 collective-permute-start.50
  968.0 10.4 collective-permute-start.51
  978.8 10.0 collective-permute-start.52
  980.7 10.4 collective-permute-start.53
  991.4 10.0 collective-permute-start.54
  993.4 10.4 collective-permute-start.55
  1004.1 10.0 collective-permute-start.56
  1006.0 10.4 collective-permute-start.57
  1016.8 10.0 collective-permute-start.58
  1018.7 10.4 collective-permute-start.59
  1029.4 10.0 collective-permute-start.60
  1031.3 10.4 collective-permute-start.61
  1042.1 10.0 collective-permute-start.62
  1044.0 10.4 collective-permute-start.63
  (14 other events, 643.2 us)
Sparse Core Ops, SparseCore 0:
  246.1 278.4 all-reduce.2
  562.9 271.7 all-reduce.4
where the time goes:
time: 1070 us; the launch traced here: 1060 us
  waiting for transfers between devices  668 us (62%)
  starting transfers between devices  333 us (31%)
  between operations  16.2 us (2%)
  other arithmetic  15.9 us (1%)
  local copies, waits for them, and re-layouts  15.4 us (1%)
  blocking collectives  12.6 us (1%)
    psum x1, waiting for transfers between devices, shards(): summed = lax.psum(product, 'mem')  279 us
    psum x1, waiting for transfers between devices, shards(): adjoint_table = lax.psum(local_table, 'mem')  272 us
    ppermute x32, starting transfers between devices, extended_2(): before = lax.ppermute(last, axis, up)  219 us
    ppermute x32, waiting for transfers between devices, extended_2(): before = lax.ppermute(last, axis, up)  109 us
    ppermute x32, starting transfers between devices, extended_2(): after = lax.ppermute(first, axis, down)  93.7 us
  transfers between devices with their start and end apart: 68, of which 35 were waited for; matrix products, arithmetic and copies ran while one was open for 1% of the time, Pallas kernels for 0%

commit v1 on v0

v1 whole, which is shorter than its diff:
```python
import math

import jax
import jax.numpy as jnp
from jax import lax
from jax.experimental import pallas as pl
from jax.experimental.pallas import tpu as pltpu
from jax.sharding import PartitionSpec as P

SWEEPS = 16
MEM = 32
TILES = 8
MESH = pl.DeviceIdType.MESH
HIGHEST = lax.Precision.HIGHEST
F32 = jnp.float32


def eye_mask(n):
    return lax.broadcasted_iota(jnp.int32, (n, n), 0) == lax.broadcasted_iota(jnp.int32, (n, n), 1)


def column(row):
    return jnp.sum(jnp.where(eye_mask(row.shape[1]), row, 0.0), axis=1, keepdims=True)


def as_row(col):
    return jnp.sum(jnp.where(eye_mask(col.shape[0]), col, 0.0), axis=0, keepdims=True)


def chunk_of(member, tile):
    return lax.rem(member // 4 + tile, TILES), lax.rem(member, 4)


def kernel(
    w_ref, p_ref, clon_ref, clat_ref, ov_ref, ow_ref, seg_ref, kind_ref, tgt_ref, cnt_ref, op_ref,
    inc_ref, back_ref,
    wbuf, lonbuf, latbuf, pbuf, pf, pin, north, south, retain,
    field, pack, packin, rs1, rs2, red1, red2, adj, fld, gbuf,
    in_send, in_recv, loc_sem, obs_send, obs_recv, out_send, out_recv,
    rs_send, rs_recv, ag_send, ag_recv, ag_own,
):
    m = lax.axis_index("mem")
    t = lax.axis_index("tile")
    scale = 1.0 / math.sqrt(MEM)

    load_p = pltpu.make_async_copy(p_ref.at[0], pin, loc_sem.at[0])
    load_p.start()
    own = [
        pltpu.make_async_copy(w_ref.at[0, t], wbuf.at[t], loc_sem.at[1]),
        pltpu.make_async_copy(clon_ref.at[t], lonbuf.at[t], loc_sem.at[2]),
        pltpu.make_async_copy(clat_ref.at[t], latbuf.at[t], loc_sem.at[3]),
    ]
    for copy in own:
        copy.start()

    barrier = pltpu.get_barrier_semaphore()
    for d in range(1, TILES):
        pl.semaphore_signal(
            barrier, inc=1, device_id=(m, lax.rem(t + d, TILES)), device_id_type=MESH
        )

    def greet(d, carry):
        pl.semaphore_signal(
            barrier, inc=1, device_id=(lax.rem(m + d, MEM), t), device_id_type=MESH
        )
        return carry

    lax.fori_loop(1, MEM, greet, 0)
    pl.semaphore_wait(barrier, TILES - 1 + MEM - 1)

    sends = []
    for a, (src, dst) in enumerate(((w_ref.at[0], wbuf), (clon_ref, lonbuf), (clat_ref, latbuf))):
        for d in range(1, TILES):
            peer = lax.rem(t + d, TILES)
            copy = pltpu.make_async_remote_copy(
                src_ref=src.at[peer], dst_ref=dst.at[t],
                send_sem=in_send.at[a, d], recv_sem=in_recv.at[a, d],
                device_id=(m, peer), device_id_type=MESH,
            )
            copy.start()
            sends.append(copy)

    load_p.wait()
    pf[...] = pin[...].astype(F32)
    psends = []
    for d in range(1, TILES):
        peer = lax.rem(t + d, TILES)
        copy = pltpu.make_async_remote_copy(
            src_ref=pf.at[peer], dst_ref=pbuf.at[t],
            send_sem=in_send.at[3, d], recv_sem=in_recv.at[3, d],
            device_id=(m, peer), device_id_type=MESH,
        )
        copy.start()
        psends.append(copy)
    own_p = pltpu.make_async_copy(pf.at[t], pbuf.at[t], loc_sem.at[4])
    own_p.start()

    slots = ov_ref.shape[0]
    live = lax.broadcasted_iota(jnp.int32, (slots, 1), 0) < cnt_ref[0]
    lane = lax.broadcasted_iota(jnp.int32, (slots, 128), 1)
    target = as_row(tgt_ref[...].astype(F32))
    seg_col = column(seg_ref[...].astype(F32))
    kind_col = column(kind_ref[...].astype(F32))
    named = (
        target == lax.broadcasted_iota(jnp.int32, (TILES, slots), 0).astype(F32)
    ).astype(F32)
    upper = (
        lax.broadcasted_iota(jnp.int32, (slots, slots), 0)
        < lax.broadcasted_iota(jnp.int32, (slots, slots), 1)
    ).astype(F32)
    earlier = jnp.dot(named, upper, preferred_element_type=F32)
    place = target * 16.0 + jnp.sum(earlier * named, axis=0, keepdims=True)
    route = (
        lax.broadcasted_iota(jnp.int32, (128, slots), 0).astype(F32) == place
    ).astype(F32)
    precision = jnp.where(live, ow_ref[...], 0.0)
    meta = jnp.where(lane == 0, seg_col, jnp.where(lane == 1, kind_col, 0.0))
    rows = jnp.concatenate([ov_ref[...], precision, meta], axis=1)
    routed = jnp.dot(route, rows, precision=HIGHEST, preferred_element_type=F32)
    pack[:, 0:16, :] = routed[:, 0:128].reshape(TILES, 16, 128)
    pack[:, 16:32, :] = routed[:, 128:256].reshape(TILES, 16, 128)
    routed_meta = routed[:, 256:384].reshape(TILES, 16, 128)
    pack[:, 32:40, :] = routed_meta[:, 0:8] + pltpu.roll(routed_meta[:, 8:16], 64, 2)
    osends = []
    for d in range(1, TILES):
        peer = lax.rem(t + d, TILES)
        copy = pltpu.make_async_remote_copy(
            src_ref=pack.at[peer], dst_ref=packin.at[t],
            send_sem=obs_send.at[d], recv_sem=obs_recv.at[d],
            device_id=(m, peer), device_id_type=MESH,
        )
        copy.start()
        osends.append(copy)
    own_o = pltpu.make_async_copy(pack.at[t], packin.at[t], loc_sem.at[5])
    own_o.start()

    for copy in own:
        copy.wait()
    for copy in sends:
        copy.wait_recv()

    row_index = lax.broadcasted_iota(jnp.int32, (128, 512), 0)
    lon = lonbuf[...].reshape(128, 512)
    lat = latbuf[...].reshape(128, 512)
    retain[...] = 1.0 - 2.0 * lon - 2.0 * lat
    north[...] = jnp.where(row_index == 0, 0.0, lat)
    south[...] = jnp.where(row_index == 127, 0.0, lat)
    field[...] = wbuf[...].reshape(128, 512)

    def sweep(step, carry):
        a = field[...]
        zonal = pltpu.roll(a, 1, 1) + pltpu.roll(a, 511, 1)
        field[...] = (
            retain[...] * a
            + lonbuf[...].reshape(128, 512) * zonal
            + north[...] * pltpu.roll(a, 1, 0)
            + south[...] * pltpu.roll(a, 127, 0)
        )
        return carry

    lax.fori_loop(0, SWEEPS, sweep, 0)
    own_p.wait()
    for copy in psends:
        copy.wait_recv()
    gbuf[...] = field[...].reshape(TILES, 16, 512) * pbuf[...]

    def add_up(index, src, rs, red, dst):
        lead, quarter = chunk_of(m, t)
        cols = pl.ds(pl.multiple_of(quarter * 128, 128), 128)

        def scatter(d, carry):
            peer = lax.rem(m + d, MEM)
            plead, pquarter = chunk_of(peer, t)
            pcols = pl.ds(pl.multiple_of(pquarter * 128, 128), 128)
            pltpu.make_async_remote_copy(
                src_ref=src.at[plead, :, pcols], dst_ref=rs.at[m],
                send_sem=rs_send.at[index], recv_sem=rs_recv.at[index],
                device_id=(peer, t), device_id_type=MESH,
            ).start()
            return carry

        lax.fori_loop(1, MEM, scatter, 0)
        rs[m] = src[lead, :, cols]
        got = rs.at[pl.ds(0, MEM - 1)]
        pltpu.make_async_copy(got, got, rs_recv.at[index]).wait()
        red[...] = jnp.sum(rs[...], axis=0)

        def spread(d, carry):
            peer = lax.rem(m + d, MEM)
            pltpu.make_async_remote_copy(
                src_ref=red, dst_ref=dst.at[t, :, cols],
                send_sem=ag_send.at[index], recv_sem=ag_recv.at[index],
                device_id=(peer, lead), device_id_type=MESH,
            ).start()
            return carry

        lax.fori_loop(1, MEM, spread, 0)

        @pl.when(lead == t)
        def _():
            pltpu.make_async_copy(red, dst.at[t, :, cols], ag_recv.at[index]).start()

        far = pltpu.make_async_remote_copy(
            src_ref=red, dst_ref=dst.at[t, :, cols],
            send_sem=ag_own.at[index], recv_sem=ag_recv.at[index],
            device_id=(m, lead), device_id_type=MESH,
        )

        @pl.when(lead != t)
        def _():
            far.start()

        pltpu.make_async_copy(dst, dst, ag_recv.at[index]).wait()
        sent = rs.at[pl.ds(0, MEM - 1)]
        pltpu.make_async_copy(sent, sent, rs_send.at[index]).wait()
        pltpu.make_async_copy(sent, sent, ag_send.at[index]).wait()

        @pl.when(lead != t)
        def _():
            far.wait_send()

    add_up(0, gbuf, rs1, red1, inc_ref)

    own_o.wait()
    for copy in osends:
        copy.wait_recv()
    value = packin[:, 0:16, :].reshape(128, 128)
    weight = packin[:, 16:32, :].reshape(128, 128)
    got = packin[:, 32:40, :]
    info = jnp.concatenate([got, pltpu.roll(got, 64, 2)], axis=1).reshape(128, 128)
    seg = info[:, 0:1]
    kind = info[:, 1:2]
    seg_row = as_row(seg)
    cell_row = lax.broadcasted_iota(jnp.int32, (128, 128), 1).astype(F32) * 4.0
    cell_col = lax.broadcasted_iota(jnp.int32, (128, 128), 0).astype(F32) * 4.0
    table = inc_ref[...]
    x = jnp.zeros((128, 128), F32)
    for q in range(4):
        pick = (seg == cell_row + float(q)).astype(F32)
        x = x + jnp.dot(
            pick, table[:, :, q * 128:(q + 1) * 128].reshape(128, 128),
            precision=HIGHEST, preferred_element_type=F32,
        )
    x = x * scale
    kinds = op_ref.shape[0]
    flat = jnp.concatenate([op_ref[k] for k in range(kinds)], axis=1)
    wide = jnp.concatenate([jnp.where(kind == float(k), x, 0.0) for k in range(kinds)], axis=1)
    modelled = lax.dot_general(
        wide, flat, (((1,), (1,)), ((), ())), precision=HIGHEST, preferred_element_type=F32
    )
    misfit = weight * (modelled - value)
    wide = jnp.concatenate([jnp.where(kind == float(k), misfit, 0.0) for k in range(kinds)], axis=1)
    z = jnp.dot(
        wide, op_ref[...].reshape(kinds * 128, 128), precision=HIGHEST, preferred_element_type=F32
    )
    for q in range(4):
        put = (seg_row == cell_col + float(q)).astype(F32)
        adj[:, :, q * 128:(q + 1) * 128] = jnp.dot(
            put, z, precision=HIGHEST, preferred_element_type=F32
        ).reshape(TILES, 16, 128)

    add_up(1, adj, rs2, red2, fld)

    field[...] = (fld[...] * pbuf[...]).reshape(128, 512)

    def sweep_back(step, carry):
        g = field[...]
        flux = lonbuf[...].reshape(128, 512) * g
        field[...] = (
            retain[...] * g
            + pltpu.roll(flux, 1, 1) + pltpu.roll(flux, 511, 1)
            + pltpu.roll(north[...] * g, 127, 0)
            + pltpu.roll(south[...] * g, 1, 0)
        )
        return carry

    lax.fori_loop(0, SWEEPS, sweep_back, 0)
    gback = wbuf
    for copy in sends:
        copy.wait_send()
    gback[...] = field[...].reshape(TILES, 16, 512)
    bsends = []
    for d in range(1, TILES):
        peer = lax.rem(t + d, TILES)
        copy = pltpu.make_async_remote_copy(
            src_ref=gback.at[peer], dst_ref=back_ref.at[t],
            send_sem=out_send.at[d], recv_sem=out_recv.at[d],
            device_id=(m, peer), device_id_type=MESH,
        )
        copy.start()
        bsends.append(copy)
    own_b = pltpu.make_async_copy(gback.at[t], back_ref.at[t], loc_sem.at[6])
    own_b.start()
    for copy in psends + osends:
        copy.wait_send()
    own_b.wait()
    for copy in bsends:
        copy.wait()


def shards(
    weights, perturb, coef_lon, coef_lat, obs_value, obs_weight,
    obs_segment, obs_kind, obs_target, obs_count, operators,
):
    scale = 1.0 / math.sqrt(MEM)
    vmem = pl.BlockSpec(memory_space=pltpu.VMEM)
    hbm = pl.BlockSpec(memory_space=pl.ANY)
    smem = pl.BlockSpec(memory_space=pltpu.SMEM)
    block = (TILES, 16, 512)
    flat = (128, 512)
    dma = pltpu.SemaphoreType.DMA
    inc, back = pl.pallas_call(
        kernel,
        out_shape=(jax.ShapeDtypeStruct(block, F32), jax.ShapeDtypeStruct(block, F32)),
        in_specs=[hbm, hbm, hbm, hbm, vmem, vmem, vmem, vmem, vmem, smem, vmem],
        out_specs=(vmem, vmem),
        scratch_shapes=[
            pltpu.VMEM(block, F32), pltpu.VMEM(block, F32), pltpu.VMEM(block, F32),
            pltpu.VMEM(block, F32), pltpu.VMEM(block, F32), pltpu.VMEM(block, jnp.bfloat16),
            pltpu.VMEM(flat, F32), pltpu.VMEM(flat, F32), pltpu.VMEM(flat, F32),
            pltpu.VMEM(flat, F32),
            pltpu.VMEM((TILES, 40, 128), F32), pltpu.VMEM((TILES, 40, 128), F32),
            pltpu.VMEM((MEM, 16, 128), F32), pltpu.VMEM((MEM, 16, 128), F32),
            pltpu.VMEM((16, 128), F32), pltpu.VMEM((16, 128), F32),
            pltpu.VMEM(block, F32), pltpu.VMEM(block, F32), pltpu.VMEM(block, F32),
            dma((4, TILES)), dma((4, TILES)), dma((7,)), dma((TILES,)), dma((TILES,)),
            dma((TILES,)), dma((TILES,)),
            dma((2,)), dma((2,)), dma((2,)), dma((2,)), dma((2,)),
        ],
        compiler_params=pltpu.CompilerParams(collective_id=0, has_side_effects=True),
    )(
        weights, perturb, coef_lon, coef_lat, obs_value, obs_weight,
        obs_segment.reshape(1, -1), obs_kind.reshape(1, -1), obs_target, obs_count, operators,
    )
    return inc * scale, weights + (back * scale)[None]


def solution(mesh):
    placed = (
        P("mem", None, "tile", None),
        P("mem", None, "tile", None),
        P(None, "tile", None),
        P(None, "tile", None),
        P(("mem", "tile"), None),
        P(("mem", "tile"), None),
        P(("mem", "tile")),
        P(("mem", "tile")),
        P(("mem", "tile"), None),
        P(("mem", "tile")),
        P(),
    )
    return jax.shard_map(
        shards,
        mesh=mesh,
        in_specs=placed,
        out_specs=(P(None, "tile", None), P("mem", None, "tile", None)),
        check_vma=False,
    )
```

time: 1070 us -> 103 us (0.10)
  the two profiles are of different devices: /device:TPU:6 before, /device:TPU:32 now
where the time goes in v1:
time: 103 us
  Pallas kernels  98 us (95%)
  other arithmetic  2.48 us (2%)
  local copies, waits for them, and re-layouts  1.37 us (1%)
  between operations  1.31 us (1%)
    pallas_call x1, Pallas kernels, shards(): pl.pallas_call(kernel, out_shape=(jax.ShapeDtypeStruct(block, F32), jax.S...  98 us

profile of v1, /device:TPU:32, one launch (start us, length us, event | category | flops | bytes accessed | tf_op | source)
XLA Modules:
  0.0 103.1 jit_solution(10941991346559899287)
XLA Ops:
  1.3 0.0 copy-start.2
  1.3 0.6 copy-done.2
  1.9 0.7 copy.13.tgt_ref
  2.6 98.0 %shard_map.122 = (f32[8,16,512]{2,1,0:T(8,128)}, f32[8,16,512]{2,1,0:T(8,128)}) custom-call(f32[1,8,16,512]{3,2,1,0:T(8,128)} %w_ref.1, bf16[1,8,16,512]{3,2,1,0:T(8,128)(2,1)} %p_ref.1, f32[8,16,512]{2,1,0:T(8,128)} %clon_ref.1, f32[8,16,512]{2,1,0:T(8,128)} %clat_ref.1, f32[64,128]{1,0:T(8,128)} %ov_ref.1, f32[64,128]{1,0:T(8,128)} %ow_ref.1, ...), custom_call_target="tpu_custom_call" | custom-call | tf_op jit(solution)/shard_map/pallas_call | solution.py:312
  100.6 0.0 copy-start
  100.7 0.0 copy-start.1
  100.7 1.7 %broadcast_multiply_fusion = f32[8,16,512]{2,1,0:T(8,128)} fusion(f32[8,16,512]{2,1,0:T(8,128)} %get-tuple-element.4), kind=kLoop, calls=%fused_computation.1 | loop fusion | flops 65536 | bytes 524288 | tf_op jit(solution)/shard_map/mul | solution.py:335
  102.4 0.0 copy-done
  102.4 0.0 copy-done.1
  102.4 0.7 bitcast_add_fusion
Async XLA Ops:
  1.3 0.7 copy-start.2
  100.6 1.8 %copy-start = (f32[1,8,16,512]{3,2,1,0:T(8,128)S(1)}, f32[1,8,16,512]{3,2,1,0:T(8,128)}, u32[]{:S(2)}) copy-start(f32[1,8,16,512]{3,2,1,0:T(8,128)} %w_ref.1) | copy-start | bytes 786436
  100.7 1.7 %copy-start.1 = (f32[8,16,512]{2,1,0:T(8,128)S(1)}, f32[8,16,512]{2,1,0:T(8,128)}, u32[]{:S(2)}) copy-start(f32[8,16,512]{2,1,0:T(8,128)} %get-tuple-element.5) | copy-start | bytes 786436

commit v2 on v1

v2 whole, which is shorter than its diff:
```python
import math

import jax
import jax.numpy as jnp
from jax import lax
from jax.experimental import pallas as pl
from jax.experimental.pallas import tpu as pltpu
from jax.sharding import PartitionSpec as P

SWEEPS = 16
MEM = 32
TILES = 8
MESH = pl.DeviceIdType.MESH
HIGHEST = lax.Precision.HIGHEST
F32 = jnp.float32
BF16 = jnp.bfloat16


def eye_mask(n):
    return lax.broadcasted_iota(jnp.int32, (n, n), 0) == lax.broadcasted_iota(jnp.int32, (n, n), 1)


def column(row):
    return jnp.sum(jnp.where(eye_mask(row.shape[1]), row, 0.0), axis=1, keepdims=True)


def as_row(col):
    return jnp.sum(jnp.where(eye_mask(col.shape[0]), col, 0.0), axis=0, keepdims=True)


def split3(x):
    hi = x.astype(BF16)
    rest = x - hi.astype(F32)
    mid = rest.astype(BF16)
    low = (rest - mid.astype(F32)).astype(BF16)
    return jnp.concatenate([hi, mid, low], axis=1)


def select(onehot, parts):
    width = parts.shape[1] // 3
    got = jnp.dot(onehot.astype(BF16), parts, preferred_element_type=F32)
    return got[:, 0:width] + got[:, width:2 * width] + got[:, 2 * width:3 * width]


def aligned(index, size):
    return pl.ds(pl.multiple_of(index * size, size), size)


def kernel(
    w_ref, p_ref, clon_ref, clat_ref, ov_ref, ow_ref, seg_ref, kind_ref, tgt_ref, cnt_ref, op_ref,
    inc_ref, back_ref,
    wbuf, coef, pbuf, pf, pin, north, south, retain, field,
    pack, lists, ad, ybuf, s2, zbuf, prod, sibp, half, rs, inc_red, adj_red, fld,
    loc_sem, snd, rcv,
):
    m = lax.axis_index("mem")
    t = lax.axis_index("tile")
    y = m // 8
    z = lax.rem(m // 2, 4)
    c = lax.rem(m, 2)
    sib = m + 1 - 2 * c
    place16 = m // 2
    scale = 1.0 / math.sqrt(MEM)
    lead = lax.rem(2 * y + z // 2 + t, TILES)
    cols = aligned(2 * c + lax.rem(z, 2), 128)

    def remote(src, dst, sem, member, tile):
        return pltpu.make_async_remote_copy(
            src_ref=src, dst_ref=dst, send_sem=snd.at[sem], recv_sem=rcv.at[sem],
            device_id=(member, tile), device_id_type=MESH,
        )

    def got(ref, sem):
        pltpu.make_async_copy(ref, ref, rcv.at[sem]).wait()

    def left(ref, sem):
        pltpu.make_async_copy(ref, ref, snd.at[sem]).wait()

    def greet(member, tile):
        pl.semaphore_signal(
            pltpu.get_barrier_semaphore(), inc=1, device_id=(member, tile), device_id_type=MESH
        )

    load_p = pltpu.make_async_copy(p_ref.at[0], pin, loc_sem.at[0])
    load_p.start()
    piece = (aligned(c, 8), aligned(y, 128))
    own = [
        pltpu.make_async_copy(w_ref.at[0, t], wbuf.at[t], loc_sem.at[1]),
        pltpu.make_async_copy(clon_ref.at[(t,) + piece], coef.at[(0, t) + piece], loc_sem.at[2]),
        pltpu.make_async_copy(clat_ref.at[(t,) + piece], coef.at[(1, t) + piece], loc_sem.at[3]),
    ]
    for copy in own:
        copy.start()

    for d in range(1, TILES):
        greet(m, lax.rem(t + d, TILES))
    greet(sib, t)

    def greet_core(d, carry):
        greet(2 * lax.rem(place16 + d, 16) + c, t)
        return carry

    lax.fori_loop(1, 16, greet_core, 0)
    for source in range(4):
        tile = lax.rem(t + 2 * y + z // 2, TILES)

        @pl.when((tile != t) | (z != source))
        def _(source=source, tile=tile):
            greet(y * 8 + source * 2 + c, tile)

    slots = ov_ref.shape[0]
    live = lax.broadcasted_iota(jnp.int32, (slots, 1), 0) < cnt_ref[0]
    lane = lax.broadcasted_iota(jnp.int32, (slots, 128), 1)
    target = tgt_ref[...].astype(F32)
    seg_col = column(seg_ref[...].astype(F32))
    kind_col = column(kind_ref[...].astype(F32))
    named = (
        target == lax.broadcasted_iota(jnp.int32, (TILES, slots), 0).astype(F32)
    ).astype(F32)
    upper = (
        lax.broadcasted_iota(jnp.int32, (slots, slots), 0)
        < lax.broadcasted_iota(jnp.int32, (slots, slots), 1)
    ).astype(F32)
    earlier = jnp.dot(named, upper, preferred_element_type=F32)
    place = target * 16.0 + jnp.sum(earlier * named, axis=0, keepdims=True)
    route = (
        lax.broadcasted_iota(jnp.int32, (128, slots), 0).astype(F32) == place
    ).astype(F32)
    precision = jnp.where(live, ow_ref[...], 0.0)
    meta = jnp.where(lane == 0, seg_col, jnp.where(lane == 1, kind_col, 0.0))
    routed = select(route, split3(jnp.concatenate([ov_ref[...], precision, meta], axis=1)))
    pack[:, 0:16, :] = routed[:, 0:128].reshape(TILES, 16, 128)
    pack[:, 16:32, :] = routed[:, 128:256].reshape(TILES, 16, 128)
    routed_meta = routed[:, 256:384].reshape(TILES, 16, 128)
    pack[:, 32:40, :] = routed_meta[:, 0:8] + pltpu.roll(routed_meta[:, 8:16], 64, 2)
    load_p.wait()
    pf[...] = pin[...].astype(F32)

    away = jnp.where((y == 0) & (z < 2), 3, 4)
    pl.semaphore_wait(pltpu.get_barrier_semaphore(), TILES - 1 + 1 + 15 + away)

    for d in range(1, TILES):
        peer = lax.rem(t + d, TILES)
        remote(clon_ref.at[(peer,) + piece], coef.at[(0, t) + piece], 0, m, peer).start()
        remote(clat_ref.at[(peer,) + piece], coef.at[(1, t) + piece], 0, m, peer).start()
    for d in range(1, TILES):
        peer = lax.rem(t + d, TILES)
        remote(pack.at[peer], lists.at[c, t], 1, m, peer).start()
    own_o = pltpu.make_async_copy(pack.at[t], lists.at[c, t], loc_sem.at[5])
    own_o.start()
    for d in range(1, TILES):
        peer = lax.rem(t + d, TILES)
        remote(w_ref.at[0, peer], wbuf.at[t], 2, m, peer).start()
    for d in range(1, TILES):
        peer = lax.rem(t + d, TILES)
        remote(pf.at[peer], pbuf.at[t], 3, m, peer).start()
    own_p = pltpu.make_async_copy(pf.at[t], pbuf.at[t], loc_sem.at[4])
    own_p.start()

    own[1].wait()
    own[2].wait()
    got(rs.at[pl.ds(0, 7)], 0)
    part = coef.at[(slice(None), slice(None)) + piece]
    for d in range(1, 4):
        remote(part, part, 4, lax.rem(y + d, 4) * 8 + z * 2 + c, t).start()

    own_o.wait()
    got(pack.at[pl.ds(0, 7)], 1)
    remote(lists.at[c], lists.at[c], 5, sib, t).start()

    got(wbuf.at[pl.ds(0, 6)], 4)
    rows8 = coef.at[:, :, piece[0], :]
    remote(rows8, rows8, 6, sib, t).start()

    got(lists.at[0], 5)

    rows = lists[...].reshape(2 * TILES, 40, 128)
    value = rows[:, 0:16].reshape(256, 128)
    weight = rows[:, 16:32].reshape(256, 128)
    info = rows[:, 32:40]
    info = jnp.concatenate([info, pltpu.roll(info, 64, 2)], axis=1).reshape(256, 128)
    kind = info[:, 1:2]
    key = as_row(info[:, 0:1] + 512.0 * kind)
    kinds = op_ref.shape[0]
    flat = op_ref[...].reshape(kinds * 128, 128)
    weighted = weight * value
    wide = jnp.concatenate([jnp.where(kind == float(k), weighted, 0.0) for k in range(kinds)], axis=1)
    pulled = jnp.dot(wide, flat, precision=HIGHEST, preferred_element_type=F32)
    weight_parts = split3(weight)
    pulled_parts = split3(pulled)
    cell = lax.broadcasted_iota(jnp.int32, (128, 256), 0)
    level = lax.rem(t - cell // 16 + TILES, TILES)
    cell = (level * 64 + lax.rem(cell, 16) * 4 + 2 * c).astype(F32)
    for b in range(2):
        every = jnp.zeros((128, 256), F32)
        span = pl.ds(b * 128, 128)
        for k in range(kinds):
            onehot = (key == cell + float(b + 512 * k)).astype(F32)
            every = every + onehot
            ad[k, :, :, span] = select(onehot, weight_parts).reshape(TILES, 16, 128)
        ad[kinds, :, :, span] = select(every, pulled_parts).reshape(TILES, 16, 128)
    for d in range(1, 4):
        there = lax.rem(y + d, 4)
        remote(
            ad.at[:, pl.ds(2 * there, 2)], ybuf.at[y], 7, there * 8 + z * 2 + c, t
        ).start()

    got(rows8, 6)
    row_index = lax.broadcasted_iota(jnp.int32, (128, 512), 0)
    lon = coef[0].reshape(128, 512)
    lat = coef[1].reshape(128, 512)
    retain[...] = 1.0 - 2.0 * lon - 2.0 * lat
    north[...] = jnp.where(row_index == 0, 0.0, lat)
    south[...] = jnp.where(row_index == 127, 0.0, lat)

    own[0].wait()
    got(wbuf.at[pl.ds(0, 7)], 2)
    field[...] = wbuf[...].reshape(128, 512)

    def sweep(step, carry):
        a = field[...]
        zonal = pltpu.roll(a, 1, 1) + pltpu.roll(a, 511, 1)
        field[...] = (
            retain[...] * a
            + coef[0].reshape(128, 512) * zonal
            + north[...] * pltpu.roll(a, 1, 0)
            + south[...] * pltpu.roll(a, 127, 0)
        )
        return carry

    lax.fori_loop(0, SWEEPS, sweep, 0)
    own_p.wait()
    got(pbuf.at[pl.ds(0, 7)], 3)
    prod[...] = field[...].reshape(TILES, 16, 512) * pbuf[...]
    mine = aligned(c, 256)
    remote(prod.at[:, :, aligned(1 - c, 256)], sibp, 8, sib, t).start()

    got(sibp, 8)
    half[...] = prod[:, :, mine] + sibp[...]

    def scatter(d, carry):
        there = lax.rem(place16 + d, 16)
        ty = there // 4
        tz = lax.rem(there, 4)
        tlead = lax.rem(2 * ty + tz // 2 + t, TILES)
        remote(
            half.at[tlead, :, aligned(lax.rem(tz, 2), 128)], rs.at[place16], 9, 2 * there + c, t
        ).start()
        return carry

    lax.fori_loop(1, 16, scatter, 0)
    rs[place16] = half[lead, :, aligned(lax.rem(z, 2), 128)]

    got(ybuf.at[pl.ds(0, 3)], 7)
    ybuf[y] = ad[:, pl.ds(2 * y, 2)]
    s2[...] = ybuf[0] + ybuf[1] + ybuf[2] + ybuf[3]
    for tz in range(4):
        level_to = lax.rem(t - 2 * y - tz // 2 + TILES, TILES)
        block = s2.at[:, tz // 2, :, pl.ds((tz % 2) * 128, 128)]
        self = (level_to == t) & (z == tz)

        @pl.when(self)
        def _(block=block):
            pltpu.make_async_copy(block, zbuf.at[z], rcv.at[10]).start()

        @pl.when(jnp.logical_not(self))
        def _(block=block, tz=tz, level_to=level_to):
            remote(block, zbuf.at[z], 10, y * 8 + tz * 2 + c, level_to).start()

    got(rs.at[pl.ds(0, 15)], 9)
    total = jnp.sum(rs[...], axis=0)
    inc_red[...] = total

    got(zbuf, 10)
    normal = zbuf[0] + zbuf[1] + zbuf[2] + zbuf[3]
    images = lax.dot_general(
        total * scale, flat, (((1,), (1,)), ((), ())), precision=HIGHEST, preferred_element_type=F32
    )
    images = images * jnp.concatenate([normal[k] for k in range(kinds)], axis=1)
    adjoint = jnp.dot(images, flat, precision=HIGHEST, preferred_element_type=F32) - normal[kinds]
    adj_red[...] = adjoint


    def spread(d, carry):
        there = lax.rem(place16 + d, 16)
        remote(adj_red, fld.at[lead, :, cols], 11, 2 * there + c, t).start()
        return carry

    lax.fori_loop(1, 16, spread, 0)
    fld[lead, :, cols] = adjoint
    got(rs.at[pl.ds(0, 15)], 11)
    side = fld.at[:, :, mine]
    remote(side, side, 12, sib, t).start()

    def tell(d, carry):
        there = lax.rem(place16 + d, 16)
        remote(inc_red, inc_ref.at[t, :, cols], 13, 2 * there + c, lead).start()
        return carry

    lax.fori_loop(1, 16, tell, 0)
    far = remote(inc_red, inc_ref.at[t, :, cols], 14, m, lead)

    @pl.when(lead == t)
    def _():
        pltpu.make_async_copy(inc_red, inc_ref.at[t, :, cols], rcv.at[14]).start()

    @pl.when(lead != t)
    def _():
        far.start()

    got(side, 12)

    field[...] = (fld[...] * pbuf[...]).reshape(128, 512)

    def sweep_back(step, carry):
        g = field[...]
        flux = coef[0].reshape(128, 512) * g
        field[...] = (
            retain[...] * g
            + pltpu.roll(flux, 1, 1) + pltpu.roll(flux, 511, 1)
            + pltpu.roll(north[...] * g, 127, 0)
            + pltpu.roll(south[...] * g, 1, 0)
        )
        return carry

    lax.fori_loop(0, SWEEPS, sweep_back, 0)
    prod_free = half
    left(prod_free, 8)
    prod[...] = field[...].reshape(TILES, 16, 512)
    for d in range(1, TILES):
        peer = lax.rem(t + d, TILES)
        remote(prod.at[peer], back_ref.at[t], 15, m, peer).start()
    own_b = pltpu.make_async_copy(prod.at[t], back_ref.at[t], loc_sem.at[6])
    own_b.start()

    got(rs.at[pl.ds(0, 15)], 13)
    got(inc_red, 14)
    side_inc = inc_ref.at[:, :, mine]
    remote(side_inc, side_inc, 16, sib, t).start()

    own_b.wait()
    got(prod.at[pl.ds(0, 7)], 15)
    got(side_inc, 16)
    left(rs.at[pl.ds(0, 7)], 0)
    left(pack.at[pl.ds(0, 7)], 1)
    left(wbuf.at[pl.ds(0, 7)], 2)
    left(pf.at[pl.ds(0, 7)], 3)
    left(wbuf.at[pl.ds(0, 6)], 4)
    left(lists.at[0], 5)
    left(rows8, 6)
    left(ybuf.at[pl.ds(0, 3)], 7)
    left(rs.at[pl.ds(0, 15)], 9)

    @pl.when((y == 0) & (z < 2))
    def _():
        left(zbuf.at[pl.ds(0, 3)], 10)

    @pl.when((y > 0) | (z >= 2))
    def _():
        left(zbuf, 10)

    left(rs.at[pl.ds(0, 15)], 11)
    left(side, 12)
    left(rs.at[pl.ds(0, 15)], 13)

    @pl.when(lead != t)
    def _():
        far.wait_send()

    left(prod.at[pl.ds(0, 7)], 15)
    left(side_inc, 16)


def shards(
    weights, perturb, coef_lon, coef_lat, obs_value, obs_weight,
    obs_segment, obs_kind, obs_target, obs_count, operators,
):
    scale = 1.0 / math.sqrt(MEM)
    vmem = pl.BlockSpec(memory_space=pltpu.VMEM)
    hbm = pl.BlockSpec(memory_space=pl.ANY)
    smem = pl.BlockSpec(memory_space=pltpu.SMEM)
    block = (TILES, 16, 512)
    flat = (128, 512)
    dma = pltpu.SemaphoreType.DMA
    inc, back = pl.pallas_call(
        kernel,
        out_shape=(jax.ShapeDtypeStruct(block, F32), jax.ShapeDtypeStruct(block, F32)),
        in_specs=[hbm, hbm, hbm, hbm, vmem, vmem, vmem, vmem, vmem, smem, vmem],
        out_specs=(vmem, vmem),
        scratch_shapes=[
            pltpu.VMEM(block, F32), pltpu.VMEM((2,) + block, F32),
            pltpu.VMEM(block, F32), pltpu.VMEM(block, F32), pltpu.VMEM(block, BF16),
            pltpu.VMEM(flat, F32), pltpu.VMEM(flat, F32), pltpu.VMEM(flat, F32),
            pltpu.VMEM(flat, F32),
            pltpu.VMEM((TILES, 40, 128), F32), pltpu.VMEM((2, TILES, 40, 128), F32),
            pltpu.VMEM((5, 8, 16, 256), F32), pltpu.VMEM((4, 5, 2, 16, 256), F32),
            pltpu.VMEM((5, 2, 16, 256), F32), pltpu.VMEM((4, 5, 16, 128), F32),
            pltpu.VMEM(block, F32), pltpu.VMEM((TILES, 16, 256), F32),
            pltpu.VMEM((TILES, 16, 256), F32), pltpu.VMEM((16, 16, 128), F32),
            pltpu.VMEM((16, 128), F32), pltpu.VMEM((16, 128), F32),
            pltpu.VMEM(block, F32),
            dma((7,)), dma((17,)), dma((17,)),
        ],
        compiler_params=pltpu.CompilerParams(collective_id=0, has_side_effects=True),
    )(
        weights, perturb, coef_lon, coef_lat, obs_value, obs_weight,
        obs_segment.reshape(1, -1), obs_kind.reshape(1, -1), obs_target.reshape(1, -1),
        obs_count, operators,
    )
    return inc * scale, weights + (back * scale)[None]


def solution(mesh):
    placed = (
        P("mem", None, "tile", None),
        P("mem", None, "tile", None),
        P(None, "tile", None),
        P(None, "tile", None),
        P(("mem", "tile"), None),
        P(("mem", "tile"), None),
        P(("mem", "tile")),
        P(("mem", "tile")),
        P(("mem", "tile"), None),
        P(("mem", "tile")),
        P(),
    )
    return jax.shard_map(
        shards,
        mesh=mesh,
        in_specs=placed,
        out_specs=(P(None, "tile", None), P("mem", None, "tile", None)),
        check_vma=False,
    )
```

time: 103 us -> 70.5 us (0.68)
  the two profiles are of different devices: /device:TPU:32 before, /device:TPU:1 now
where the time goes in v2:
time: 70.5 us; the launch traced here: 70 us
  Pallas kernels  66.2 us (94%)
  other arithmetic  2.48 us (4%)
  between operations  1.31 us (2%)
    pallas_call x1, Pallas kernels, shards(): pl.pallas_call(kernel, out_shape=(jax.ShapeDtypeStruct(block, F32), jax.S...  66.2 us
    mul x1, other arithmetic, shards(): return (inc * scale, weights + (back * scale)[None])  1.73 us

profile of v2, /device:TPU:1, one launch (start us, length us, event | category | flops | bytes accessed | tf_op | source)
XLA Modules:
  0.0 70.0 jit_solution(6273363466210127031)
XLA Ops:
  1.3 66.2 %shard_map.122 = (f32[8,16,512]{2,1,0:T(8,128)}, f32[8,16,512]{2,1,0:T(8,128)}) custom-call(f32[1,8,16,512]{3,2,1,0:T(8,128)} %w_ref.1, bf16[1,8,16,512]{3,2,1,0:T(8,128)(2,1)} %p_ref.1, f32[8,16,512]{2,1,0:T(8,128)} %clon_ref.1, f32[8,16,512]{2,1,0:T(8,128)} %clat_ref.1, f32[64,128]{1,0:T(8,128)} %ov_ref.1, f32[64,128]{1,0:T(8,128)} %ow_ref.1, ...), custom_call_target="tpu_custom_call" | custom-call | tf_op jit(solution)/shard_map/pallas_call | solution.py:385
  67.5 0.0 copy-start
  67.5 0.0 copy-start.1
  67.5 1.7 %broadcast_multiply_fusion = f32[8,16,512]{2,1,0:T(8,128)} fusion(f32[8,16,512]{2,1,0:T(8,128)} %get-tuple-element.4), kind=kLoop, calls=%fused_computation.1 | loop fusion | flops 65536 | bytes 524288 | tf_op jit(solution)/shard_map/mul | solution.py:410
  69.2 0.0 copy-done
  69.2 0.0 copy-done.1
  69.2 0.7 %bitcast_add_fusion = f32[1,8,16,512]{3,2,1,0:T(8,128)} fusion(f32[1,8,16,512]{3,2,1,0:T(8,128)S(1)} %copy-done, f32[8,16,512]{2,1,0:T(8,128)S(1)} %copy-done.1), kind=kLoop, calls=%fused_computation | loop fusion | flops 131072 | bytes 786432 | tf_op jit(solution)/shard_map/add | solution.py:410
Async XLA Ops:
  67.5 1.8 %copy-start = (f32[1,8,16,512]{3,2,1,0:T(8,128)S(1)}, f32[1,8,16,512]{3,2,1,0:T(8,128)}, u32[]{:S(2)}) copy-start(f32[1,8,16,512]{3,2,1,0:T(8,128)} %w_ref.1) | copy-start | bytes 786436
  67.5 1.7 %copy-start.1 = (f32[8,16,512]{2,1,0:T(8,128)S(1)}, f32[8,16,512]{2,1,0:T(8,128)}, u32[]{:S(2)}) copy-start(f32[8,16,512]{2,1,0:T(8,128)} %get-tuple-element.5) | copy-start | bytes 786436

commit v3 on v2

v3 whole, which is shorter than its diff:
```python
import math

import jax
import jax.numpy as jnp
from jax import lax
from jax.experimental import pallas as pl
from jax.experimental.pallas import tpu as pltpu
from jax.sharding import PartitionSpec as P

SWEEPS = 16
AROUND = (5, 3, 7, 1, 4, 2, 6)
VMEM_LIMIT = 24 * 1024 * 1024
MEM = 32
TILES = 8
MESH = pl.DeviceIdType.MESH
HIGHEST = lax.Precision.HIGHEST
F32 = jnp.float32
BF16 = jnp.bfloat16


def eye_mask(n):
    return lax.broadcasted_iota(jnp.int32, (n, n), 0) == lax.broadcasted_iota(jnp.int32, (n, n), 1)


def column(row):
    return jnp.sum(jnp.where(eye_mask(row.shape[1]), row, 0.0), axis=1, keepdims=True)


def as_row(col):
    return jnp.sum(jnp.where(eye_mask(col.shape[0]), col, 0.0), axis=0, keepdims=True)


def split3(x):
    hi = x.astype(BF16)
    rest = x - hi.astype(F32)
    mid = rest.astype(BF16)
    low = (rest - mid.astype(F32)).astype(BF16)
    return jnp.concatenate([hi, mid, low], axis=1)


def select(onehot, parts):
    width = parts.shape[1] // 3
    got = jnp.dot(onehot.astype(BF16), parts, preferred_element_type=F32)
    return got[:, 0:width] + got[:, width:2 * width] + got[:, 2 * width:3 * width]


def aligned(index, size):
    return pl.ds(pl.multiple_of(index * size, size), size)


def kernel(
    cnt_ref, w_ref, p_ref, clon_ref, clat_ref, ov_hbm, ow_hbm, seg_hbm, kind_hbm, tgt_hbm, op_hbm,
    both_ref,
    wbuf, coef, pbuf, pf, pin, retain, ov_ref, ow_ref, op_ref, seg_ref, kind_ref, tgt_ref,
    pack, lists, ad, ybuf, s2, zbuf, prod, sibp, half, rs, inc_red, adj_red, fld,
    loc_sem, snd, rcv, list_rcv,
):
    inc_ref, back_ref = both_ref.at[0], both_ref.at[1]
    m = lax.axis_index("mem")
    t = lax.axis_index("tile")
    y = m // 8
    z = lax.rem(m // 2, 4)
    c = lax.rem(m, 2)
    sib = m + 1 - 2 * c
    place16 = m // 2
    scale = 1.0 / math.sqrt(MEM)
    lead = lax.rem(2 * y + z // 2 + t, TILES)
    cols = aligned(2 * c + lax.rem(z, 2), 128)

    def remote(src, dst, sem, member, tile):
        return pltpu.make_async_remote_copy(
            src_ref=src, dst_ref=dst, send_sem=snd.at[sem], recv_sem=rcv.at[sem],
            device_id=(member, tile), device_id_type=MESH,
        )

    def got(ref, sem):
        pltpu.make_async_copy(ref, ref, rcv.at[sem]).wait()

    def left(ref, sem):
        pltpu.make_async_copy(ref, ref, snd.at[sem]).wait()

    def greet(member, tile):
        pl.semaphore_signal(
            pltpu.get_barrier_semaphore(), inc=1, device_id=(member, tile), device_id_type=MESH
        )

    for d in range(1, TILES):
        greet(m, lax.rem(t + d, TILES))
    greet(sib, t)

    def greet_core(d, carry):
        greet(2 * lax.rem(place16 + d, 16) + c, t)
        return carry

    lax.fori_loop(1, 16, greet_core, 0)
    for source in range(4):
        tile = lax.rem(t + 2 * y + z // 2, TILES)

        @pl.when((tile != t) | (z != source))
        def _(source=source, tile=tile):
            greet(y * 8 + source * 2 + c, tile)

    piece = (aligned(c, 8), aligned(y, 128))
    loads = [
        pltpu.make_async_copy(seg_hbm, seg_ref, loc_sem.at[10]),
        pltpu.make_async_copy(kind_hbm, kind_ref, loc_sem.at[11]),
        pltpu.make_async_copy(tgt_hbm, tgt_ref, loc_sem.at[12]),
        pltpu.make_async_copy(op_hbm, op_ref, loc_sem.at[7]),
        pltpu.make_async_copy(ov_hbm, ov_ref, loc_sem.at[8]),
        pltpu.make_async_copy(ow_hbm, ow_ref, loc_sem.at[9]),
        pltpu.make_async_copy(p_ref.at[0], pin, loc_sem.at[0]),
    ]
    own = [
        pltpu.make_async_copy(clon_ref.at[(t,) + piece], coef.at[(0, t) + piece], loc_sem.at[2]),
        pltpu.make_async_copy(clat_ref.at[(t,) + piece], coef.at[(1, t) + piece], loc_sem.at[3]),
        pltpu.make_async_copy(w_ref.at[0, t], wbuf.at[t], loc_sem.at[1]),
    ]
    for copy in loads + own:
        copy.start()

    slots = ov_ref.shape[0]
    kinds = op_ref.shape[0]
    live = lax.broadcasted_iota(jnp.int32, (slots, 1), 0) < cnt_ref[0]
    lane = lax.broadcasted_iota(jnp.int32, (slots, 128), 1)
    for copy in loads[:3]:
        copy.wait()
    target = tgt_ref[...].astype(F32)
    seg_col = column(seg_ref[...].astype(F32))
    kind_col = column(kind_ref[...].astype(F32))
    named = (
        target == lax.broadcasted_iota(jnp.int32, (TILES, slots), 0).astype(F32)
    ).astype(F32)
    upper = (
        lax.broadcasted_iota(jnp.int32, (slots, slots), 0)
        < lax.broadcasted_iota(jnp.int32, (slots, slots), 1)
    ).astype(F32)
    earlier = jnp.dot(named, upper, preferred_element_type=F32)
    place = target * 16.0 + jnp.sum(earlier * named, axis=0, keepdims=True)
    route = (
        lax.broadcasted_iota(jnp.int32, (128, slots), 0).astype(F32) == place
    ).astype(F32)
    for copy in loads[3:]:
        copy.wait()
    flat = op_ref[...].reshape(kinds * 128, 128)
    precision = jnp.where(live, ow_ref[...], 0.0)
    weighted = precision * ov_ref[...]
    wide = jnp.concatenate(
        [jnp.where(kind_col == float(k), weighted, 0.0) for k in range(kinds)], axis=1
    )
    pulled = jnp.dot(wide, flat, precision=HIGHEST, preferred_element_type=F32)
    meta = jnp.where(lane == 0, seg_col, jnp.where(lane == 1, kind_col, 0.0))
    routed = select(route, split3(jnp.concatenate([pulled, precision, meta], axis=1)))
    pack[:, 0:16, :] = routed[:, 0:128].reshape(TILES, 16, 128)
    pack[:, 16:32, :] = routed[:, 128:256].reshape(TILES, 16, 128)
    routed_meta = routed[:, 256:384].reshape(TILES, 16, 128)
    pack[:, 32:40, :] = routed_meta[:, 0:8] + pltpu.roll(routed_meta[:, 8:16], 64, 2)
    pf[...] = pin[...].astype(F32)

    away = jnp.where((y == 0) & (z < 2), 3, 4)
    pl.semaphore_wait(pltpu.get_barrier_semaphore(), TILES - 1 + 1 + 15 + away)

    for d in AROUND:
        peer = lax.rem(t + d, TILES)
        remote(clon_ref.at[(peer,) + piece], coef.at[(0, t) + piece], 0, m, peer).start()
        remote(clat_ref.at[(peer,) + piece], coef.at[(1, t) + piece], 0, m, peer).start()
    for d in AROUND:
        peer = lax.rem(t + d, TILES)
        pltpu.make_async_remote_copy(
            src_ref=pack.at[peer], dst_ref=lists.at[c, t],
            send_sem=snd.at[1], recv_sem=list_rcv.at[d],
            device_id=(m, peer), device_id_type=MESH,
        ).start()
    own_o = pltpu.make_async_copy(pack.at[t], lists.at[c, t], loc_sem.at[5])
    own_o.start()
    for d in AROUND:
        peer = lax.rem(t + d, TILES)
        remote(w_ref.at[0, peer], wbuf.at[t], 2, m, peer).start()
    own[0].wait()
    own[1].wait()
    got(rs.at[pl.ds(0, 7)], 0)
    part = coef.at[(slice(None), slice(None)) + piece]
    for d in (2, 1, 3):
        remote(part, part, 4, lax.rem(y + d, 4) * 8 + z * 2 + c, t).start()

    own_o.wait()
    remote(lists.at[c, t], lists.at[c, t], 5, sib, t).start()
    for d in (4, 2, 6, 7, 1, 3, 5):
        source = lax.rem(t + TILES - d, TILES)
        block = lists.at[c, source]
        pltpu.make_async_copy(block, block, list_rcv.at[d]).wait()
        remote(block, block, 5, sib, t).start()

    for d in AROUND:
        peer = lax.rem(t + d, TILES)
        remote(pf.at[peer], pbuf.at[t], 3, m, peer).start()
    own_p = pltpu.make_async_copy(pf.at[t], pbuf.at[t], loc_sem.at[4])
    own_p.start()

    got(lists.at[0], 5)

    rows = lists[...].reshape(2 * TILES, 40, 128)
    pulled_parts = split3(rows[:, 0:16].reshape(256, 128))
    weight_parts = split3(rows[:, 16:32].reshape(256, 128))
    info = rows[:, 32:40]
    info = jnp.concatenate([info, pltpu.roll(info, 64, 2)], axis=1).reshape(256, 128)
    seg_row = as_row(info[:, 0:1])
    key_row = seg_row + 512.0 * as_row(info[:, 1:2])
    row = lax.broadcasted_iota(jnp.int32, (256, 256), 0)
    fixed = lax.rem(row, 16) * 4 + 2 * c + lax.rem(row // 32, 2)
    for d in (2, 1, 3, 0):
        there = lax.rem(y + d, 4)
        level = lax.rem(t - 2 * there - lax.rem(row // 16, 2) + TILES, TILES)
        cell = fixed + level * 64
        each = select(
            (key_row == (cell + (row // 64) * 512).astype(F32)).astype(F32), weight_parts
        ).reshape(kinds, 2, 2, 16, 128)
        every = select(
            (seg_row == cell[0:64].astype(F32)).astype(F32), pulled_parts
        ).reshape(2, 2, 16, 128)
        for b in range(2):
            span = pl.ds(b * 128, 128)
            for near in range(2):
                ad[d, near, 0:kinds, :, span] = each[:, b, near]
                ad[d, near, kinds, :, span] = every[b, near]
        if d:
            remote(ad.at[d, 0], ybuf.at[0, d - 1], 7, there * 8 + z * 2 + c, t).start()
    for d in (2, 1, 3):
        there = lax.rem(y + d, 4)
        remote(ad.at[d, 1], ybuf.at[1, d - 1], 17, there * 8 + z * 2 + c, t).start()

    got(wbuf.at[pl.ds(0, 6)], 4)
    rows8 = coef.at[:, :, piece[0], :]
    remote(rows8, rows8, 6, sib, t).start()

    got(rows8, 6)
    retain[...] = 1.0 - 2.0 * coef[0] - 2.0 * coef[1]

    own[2].wait()
    got(pf.at[pl.ds(0, 7)], 2)

    top = lax.broadcasted_iota(jnp.int32, (8, 512), 0) == 0
    bottom = lax.broadcasted_iota(jnp.int32, (8, 512), 0) == 7
    nothing = jnp.zeros((8, 512), F32)

    def block_of(i):
        return i // 2, pl.ds((i % 2) * 8, 8)

    def sweep(step, carry):
        here = wbuf[block_of(0)]
        down_before, up = nothing, pltpu.roll(here, 7, 0)
        for i in range(16):
            place = block_of(i)
            after = wbuf[block_of(i + 1)] if i < 15 else nothing
            down = pltpu.roll(here, 1, 0)
            up_after = pltpu.roll(after, 7, 0)
            across = jnp.where(top, down_before, down) + jnp.where(bottom, up_after, up)
            zonal = pltpu.roll(here, 1, 1) + pltpu.roll(here, 511, 1)
            wbuf[place] = (
                retain[place] * here + coef[(0,) + place] * zonal + coef[(1,) + place] * across
            )
            here, down_before, up = after, down, up_after
        return carry

    lax.fori_loop(0, SWEEPS, sweep, 0, unroll=4)
    def pass_on(near, sem):
        got(ybuf.at[near], sem)
        s2[near] = ad[0, near] + ybuf[near, 0] + ybuf[near, 1] + ybuf[near, 2]
        level_to = lax.rem(t - 2 * y - near + TILES, TILES)
        for b in range(2):
            tz = 2 * near + b
            block = s2.at[near, :, :, pl.ds(b * 128, 128)]
            self = (level_to == t) & (z == tz)

            @pl.when(self)
            def _(block=block):
                pltpu.make_async_copy(block, zbuf.at[z], rcv.at[10]).start()

            @pl.when(jnp.logical_not(self))
            def _(block=block, tz=tz):
                remote(block, zbuf.at[z], 10, y * 8 + tz * 2 + c, level_to).start()

    own_p.wait()
    got(pbuf.at[pl.ds(0, 7)], 3)
    prod[...] = wbuf[...] * pbuf[...]
    mine = aligned(c, 256)
    remote(prod.at[:, :, aligned(1 - c, 256)], sibp, 8, sib, t).start()

    pass_on(0, 7)
    got(sibp, 8)
    half[...] = prod[:, :, mine] + sibp[...]

    def scatter(d, carry):
        there = lax.rem(place16 + d, 16)
        ty = there // 4
        tz = lax.rem(there, 4)
        tlead = lax.rem(2 * ty + tz // 2 + t, TILES)
        remote(
            half.at[tlead, :, aligned(lax.rem(tz, 2), 128)], rs.at[d - 1], 9, 2 * there + c, t
        ).start()
        return carry

    lax.fori_loop(1, 16, scatter, 0)

    pass_on(1, 17)

    got(rs, 9)
    total = half[lead, :, aligned(lax.rem(z, 2), 128)] + jnp.sum(rs[...], axis=0)
    inc_red[...] = total

    got(zbuf, 10)
    normal = zbuf[0] + zbuf[1] + zbuf[2] + zbuf[3]
    images = lax.dot_general(
        total * scale, flat, (((1,), (1,)), ((), ())), precision=HIGHEST, preferred_element_type=F32
    )
    images = images * jnp.concatenate([normal[k] for k in range(kinds)], axis=1)
    adjoint = jnp.dot(images, flat, precision=HIGHEST, preferred_element_type=F32) - normal[kinds]
    adj_red[...] = adjoint


    def spread(d, carry):
        there = lax.rem(place16 + d, 16)
        remote(adj_red, fld.at[lead, :, cols], 11, 2 * there + c, t).start()
        return carry

    lax.fori_loop(1, 16, spread, 0)
    fld[lead, :, cols] = adjoint
    got(rs, 11)
    side = fld.at[:, :, mine]
    remote(side, side, 12, sib, t).start()

    def tell(d, carry):
        there = lax.rem(place16 + d, 16)
        remote(inc_red, inc_ref.at[t, :, cols], 13, 2 * there + c, lead).start()
        return carry

    lax.fori_loop(1, 16, tell, 0)
    far = remote(inc_red, inc_ref.at[t, :, cols], 14, m, lead)

    @pl.when(lead == t)
    def _():
        pltpu.make_async_copy(inc_red, inc_ref.at[t, :, cols], rcv.at[14]).start()

    @pl.when(lead != t)
    def _():
        far.start()

    got(side, 12)

    left(sibp, 8)
    prod[...] = fld[...] * pbuf[...]

    def sweep_back(step, carry):
        here = prod[block_of(0)]
        flux = coef[(1,) + block_of(0)] * here
        down_before, up = nothing, pltpu.roll(flux, 7, 0)
        for i in range(16):
            place = block_of(i)
            if i < 15:
                after = prod[block_of(i + 1)]
                flux_after = coef[(1,) + block_of(i + 1)] * after
            else:
                after = flux_after = nothing
            down = pltpu.roll(flux, 1, 0)
            up_after = pltpu.roll(flux_after, 7, 0)
            across = jnp.where(top, down_before, down) + jnp.where(bottom, up_after, up)
            flux_lon = coef[(0,) + place] * here
            prod[place] = (
                retain[place] * here
                + (pltpu.roll(flux_lon, 1, 1) + pltpu.roll(flux_lon, 511, 1))
                + across
            )
            here, flux, down_before, up = after, flux_after, down, up_after
        return carry

    lax.fori_loop(0, SWEEPS, sweep_back, 0, unroll=4)
    for d in AROUND:
        peer = lax.rem(t + d, TILES)
        remote(prod.at[peer], back_ref.at[t], 15, m, peer).start()
    own_b = pltpu.make_async_copy(prod.at[t], back_ref.at[t], loc_sem.at[6])
    own_b.start()

    got(rs, 13)
    got(inc_red, 14)
    side_inc = inc_ref.at[:, :, mine]
    remote(side_inc, side_inc, 16, sib, t).start()

    own_b.wait()
    got(prod.at[pl.ds(0, 7)], 15)
    got(side_inc, 16)
    left(rs.at[pl.ds(0, 7)], 0)
    left(pack.at[pl.ds(0, 7)], 1)
    left(wbuf.at[pl.ds(0, 7)], 2)
    left(pf.at[pl.ds(0, 7)], 3)
    left(wbuf.at[pl.ds(0, 6)], 4)
    left(lists.at[0], 5)
    left(rows8, 6)
    left(ybuf.at[0], 7)
    left(ybuf.at[1], 17)
    left(rs, 9)

    @pl.when((y == 0) & (z < 2))
    def _():
        left(zbuf.at[pl.ds(0, 3)], 10)

    @pl.when((y > 0) | (z >= 2))
    def _():
        left(zbuf, 10)

    left(rs, 11)
    left(side, 12)
    left(rs, 13)

    @pl.when(lead != t)
    def _():
        far.wait_send()

    left(prod.at[pl.ds(0, 7)], 15)
    left(side_inc, 16)


def shards(
    weights, perturb, coef_lon, coef_lat, obs_value, obs_weight,
    obs_segment, obs_kind, obs_target, obs_count, operators,
):
    scale = 1.0 / math.sqrt(MEM)
    hbm = pl.BlockSpec(memory_space=pl.ANY)
    smem = pl.BlockSpec(memory_space=pltpu.SMEM)
    block = (TILES, 16, 512)
    dma = pltpu.SemaphoreType.DMA
    far = pl.BlockSpec(memory_space=pltpu.HBM)
    given = [
        pltpu.with_memory_space_constraint(a, pltpu.HBM)
        for a in (
            weights, perturb, coef_lon, coef_lat, obs_value, obs_weight,
            obs_segment.reshape(1, -1), obs_kind.reshape(1, -1), obs_target.reshape(1, -1), operators,
        )
    ]
    both = pl.pallas_call(
        kernel,
        out_shape=jax.ShapeDtypeStruct((2,) + block, F32),
        in_specs=[smem] + [far] * len(given),
        out_specs=hbm,
        scratch_shapes=[
            pltpu.VMEM(block, F32), pltpu.VMEM((2,) + block, F32),
            pltpu.VMEM(block, F32), pltpu.VMEM(block, F32), pltpu.VMEM(block, BF16),
            pltpu.VMEM(block, F32), pltpu.VMEM(obs_value.shape, F32),
            pltpu.VMEM(obs_weight.shape, F32), pltpu.VMEM(operators.shape, F32),
            pltpu.VMEM((1, obs_segment.shape[0]), jnp.int32),
            pltpu.VMEM((1, obs_kind.shape[0]), jnp.int32),
            pltpu.VMEM((1, obs_target.shape[0]), jnp.int32),
            pltpu.VMEM((TILES, 40, 128), F32), pltpu.VMEM((2, TILES, 40, 128), F32),
            pltpu.VMEM((4, 2, 5, 16, 256), F32), pltpu.VMEM((2, 3, 5, 16, 256), F32),
            pltpu.VMEM((2, 5, 16, 256), F32), pltpu.VMEM((4, 5, 16, 128), F32),
            pltpu.VMEM(block, F32), pltpu.VMEM((TILES, 16, 256), F32),
            pltpu.VMEM((TILES, 16, 256), F32), pltpu.VMEM((15, 16, 128), F32),
            pltpu.VMEM((16, 128), F32), pltpu.VMEM((16, 128), F32),
            pltpu.VMEM(block, F32),
            dma((13,)), dma((18,)), dma((18,)), dma((TILES,)),
        ],
        compiler_params=pltpu.CompilerParams(
            collective_id=0, has_side_effects=True, vmem_limit_bytes=VMEM_LIMIT
        ),
    )(obs_count, *given)
    return both[0] * scale, weights + (both[1] * scale)[None]


def solution(mesh):
    placed = (
        P("mem", None, "tile", None),
        P("mem", None, "tile", None),
        P(None, "tile", None),
        P(None, "tile", None),
        P(("mem", "tile"), None),
        P(("mem", "tile"), None),
        P(("mem", "tile")),
        P(("mem", "tile")),
        P(("mem", "tile"), None),
        P(("mem", "tile")),
        P(),
    )
    return jax.shard_map(
        shards,
        mesh=mesh,
        in_specs=placed,
        out_specs=(P(None, "tile", None), P("mem", None, "tile", None)),
        check_vma=False,
    )
```

time: 70.5 us -> 66.1 us (0.938)
  Pallas kernels: 66.2 us -> 63.8 us
  other arithmetic: 2.48 us -> 0.87 us
    pallas_call x1, Pallas kernels: 66.2 us -> 63.8 us  [shards(): pl.pallas_call(kernel, out_shape=jax.ShapeDtypeStruct((2,) + block, F32),...]
    mul x1 -> x0, other arithmetic: 1.73 us -> none  [shards(): return (inc * scale, weights + (back * scale)[None])]
where the time goes in v3:
time: 66.1 us; the launch traced here: 66 us
  Pallas kernels  63.8 us (97%)
  between operations  1.3 us (2%)
  other arithmetic  0.87 us (1%)
    pallas_call x1, Pallas kernels, shards(): pl.pallas_call(kernel, out_shape=jax.ShapeDtypeStruct((2,) + block, F32),...  63.8 us

profile of v3, /device:TPU:1, one launch (start us, length us, event | category | flops | bytes accessed | tf_op | source)
XLA Modules:
  0.0 66.0 jit_solution(1613567216368316428)
XLA Ops:
  1.3 0.0 copy-start
  1.3 63.8 %shard_map.122 = f32[2,8,16,512]{3,2,1,0:T(8,128)S(1)} custom-call(s32[1]{0:T(128)S(6)} %copy.13.cnt_ref, f32[1,8,16,512]{3,2,1,0:T(8,128)} %w_ref.1, bf16[1,8,16,512]{3,2,1,0:T(8,128)(2,1)} %p_ref.1, f32[8,16,512]{2,1,0:T(8,128)} %clon_ref.1, f32[8,16,512]{2,1,0:T(8,128)} %clat_ref.1, f32[64,128]{1,0:T(8,128)} %ov_hbm.1, f32[64,128]{1,0:T(8,128)} %ow_hbm.1, ...), custom_call_target="tpu_custom_call" | custom-call | tf_op jit(solution)/shard_map/pallas_call | solution.py:438
  65.1 0.0 copy-done
  65.1 0.9 %multiply_add_fusion = (f32[1,8,16,512]{3,2,1,0:T(8,128)}, f32[8,16,512]{2,1,0:T(8,128)}) fusion(f32[1,8,16,512]{3,2,1,0:T(8,128)S(1)} %copy-done, f32[2,8,16,512]{3,2,1,0:T(8,128)S(1)} %shard_map.122), kind=kLoop, calls=%fused_computation | loop fusion | flops 196608 | bytes 1310720 | tf_op jit(solution)/shard_map/add | solution.py:464
Async XLA Ops:
  1.3 63.8 %copy-start = (f32[1,8,16,512]{3,2,1,0:T(8,128)S(1)}, f32[1,8,16,512]{3,2,1,0:T(8,128)}, u32[]{:S(2)}) copy-start(f32[1,8,16,512]{3,2,1,0:T(8,128)} %w_ref.1) | copy-start | bytes 786436

commit v4 on v3

--- a/solution.py
+++ b/solution.py
@@ -52,7 +52,7 @@
     cnt_ref, w_ref, p_ref, clon_ref, clat_ref, ov_hbm, ow_hbm, seg_hbm, kind_hbm, tgt_hbm, op_hbm,
     both_ref,
     wbuf, coef, pbuf, pf, pin, retain, ov_ref, ow_ref, op_ref, seg_ref, kind_ref, tgt_ref,
-    pack, lists, ad, ybuf, s2, zbuf, prod, sibp, half, rs, inc_red, adj_red, fld,
+    pack, lists, ad, ybuf, s2, zbuf, prod, sibp, half, rsy, sumy, rsz, rs, inc_red, adj_red, fld,
     loc_sem, snd, rcv, list_rcv,
 ):
     inc_ref, back_ref = both_ref.at[0], both_ref.at[1]
@@ -287,24 +287,25 @@
 
     pass_on(0, 7)
     got(sibp, 8)
-    half[...] = prod[:, :, mine] + sibp[...]
-
-    def scatter(d, carry):
-        there = lax.rem(place16 + d, 16)
-        ty = there // 4
-        tz = lax.rem(there, 4)
-        tlead = lax.rem(2 * ty + tz // 2 + t, TILES)
+    for near in range(8):
+        tile_to = lax.rem(near + t, TILES)
+        half[near] = prod[tile_to, :, mine] + sibp[tile_to]
+    for d in (2, 1, 3):
+        there = lax.rem(y + d, 4)
+        remote(half.at[pl.ds(2 * there, 2)], rsy.at[d - 1], 9, there * 8 + z * 2 + c, t).start()
+
+    pass_on(1, 17)
+
+    got(rsy, 9)
+    sumy[...] = half[pl.ds(2 * y, 2)] + rsy[0] + rsy[1] + rsy[2]
+    for d in (2, 1, 3):
+        tz = lax.rem(z + d, 4)
         remote(
-            half.at[tlead, :, aligned(lax.rem(tz, 2), 128)], rs.at[d - 1], 9, 2 * there + c, t
+            sumy.at[tz // 2, :, aligned(lax.rem(tz, 2), 128)], rsz.at[d - 1], 18,
+            y * 8 + tz * 2 + c, t,
         ).start()
-        return carry
-
-    lax.fori_loop(1, 16, scatter, 0)
-
-    pass_on(1, 17)
-
-    got(rs, 9)
-    total = half[lead, :, aligned(lax.rem(z, 2), 128)] + jnp.sum(rs[...], axis=0)
+    got(rsz, 18)
+    total = sumy[z // 2, :, aligned(lax.rem(z, 2), 128)] + rsz[0] + rsz[1] + rsz[2]
     inc_red[...] = total
 
     got(zbuf, 10)
@@ -324,25 +325,22 @@
 
     lax.fori_loop(1, 16, spread, 0)
     fld[lead, :, cols] = adjoint
+    for d in (2, 1, 3):
+        tz = lax.rem(z + d, 4)
+        remote(inc_red, inc_ref.at[t, :, cols], 13, y * 8 + tz * 2 + c, lead).start()
+    far = remote(inc_red, inc_ref.at[t, :, cols], 14, m, lead)
+
+    @pl.when(lead == t)
+    def _():
+        pltpu.make_async_copy(inc_red, inc_ref.at[t, :, cols], rcv.at[14]).start()
+
+    @pl.when(lead != t)
+    def _():
+        far.start()
+
     got(rs, 11)
     side = fld.at[:, :, mine]
     remote(side, side, 12, sib, t).start()
-
-    def tell(d, carry):
-        there = lax.rem(place16 + d, 16)
-        remote(inc_red, inc_ref.at[t, :, cols], 13, 2 * there + c, lead).start()
-        return carry
-
-    lax.fori_loop(1, 16, tell, 0)
-    far = remote(inc_red, inc_ref.at[t, :, cols], 14, m, lead)
-
-    @pl.when(lead == t)
-    def _():
-        pltpu.make_async_copy(inc_red, inc_ref.at[t, :, cols], rcv.at[14]).start()
-
-    @pl.when(lead != t)
-    def _():
-        far.start()
 
     got(side, 12)
 
@@ -379,8 +377,13 @@
     own_b = pltpu.make_async_copy(prod.at[t], back_ref.at[t], loc_sem.at[6])
     own_b.start()
 
-    got(rs, 13)
+    got(rsz, 13)
     got(inc_red, 14)
+    for near in range(2):
+        block = inc_ref.at[lax.rem(t - 2 * y - near + TILES, TILES), :, mine]
+        for d in (2, 1, 3):
+            remote(block, block, 19, lax.rem(y + d, 4) * 8 + z * 2 + c, t).start()
+    got(half.at[pl.ds(0, 6)], 19)
     side_inc = inc_ref.at[:, :, mine]
     remote(side_inc, side_inc, 16, sib, t).start()
 
@@ -396,7 +399,8 @@
     left(rows8, 6)
     left(ybuf.at[0], 7)
     left(ybuf.at[1], 17)
-    left(rs, 9)
+    left(rsy, 9)
+    left(rsz, 18)
 
     @pl.when((y == 0) & (z < 2))
     def _():
@@ -408,7 +412,8 @@
 
     left(rs, 11)
     left(side, 12)
-    left(rs, 13)
+    left(rsz, 13)
+    left(half.at[pl.ds(0, 6)], 19)
 
     @pl.when(lead != t)
     def _():
@@ -452,10 +457,12 @@
             pltpu.VMEM((4, 2, 5, 16, 256), F32), pltpu.VMEM((2, 3, 5, 16, 256), F32),
             pltpu.VMEM((2, 5, 16, 256), F32), pltpu.VMEM((4, 5, 16, 128), F32),
             pltpu.VMEM(block, F32), pltpu.VMEM((TILES, 16, 256), F32),
-            pltpu.VMEM((TILES, 16, 256), F32), pltpu.VMEM((15, 16, 128), F32),
+            pltpu.VMEM((TILES, 16, 256), F32), pltpu.VMEM((3, 2, 16, 256), F32),
+            pltpu.VMEM((2, 16, 256), F32), pltpu.VMEM((3, 16, 128), F32),
+            pltpu.VMEM((15, 16, 128), F32),
             pltpu.VMEM((16, 128), F32), pltpu.VMEM((16, 128), F32),
             pltpu.VMEM(block, F32),
-            dma((13,)), dma((18,)), dma((18,)), dma((TILES,)),
+            dma((13,)), dma((20,)), dma((20,)), dma((TILES,)),
         ],
         compiler_params=pltpu.CompilerParams(
             collective_id=0, has_side_effects=True, vmem_limit_bytes=VMEM_LIMIT

time: 66.1 us -> 62.5 us (0.946)
  Pallas kernels: 63.8 us -> 60.2 us
    pallas_call x1, Pallas kernels: 63.8 us -> 60.2 us  [shards(): pl.pallas_call(kernel, out_shape=jax.ShapeDtypeStruct((2,) + block, F32),...]
where the time goes in v4:
time: 62.5 us; the launch traced here: 62.4 us
  Pallas kernels  60.2 us (96%)
  between operations  1.3 us (2%)
  other arithmetic  0.87 us (1%)
    pallas_call x1, Pallas kernels, shards(): pl.pallas_call(kernel, out_shape=jax.ShapeDtypeStruct((2,) + block, F32),...  60.2 us

profile of v4, /device:TPU:1, one launch (start us, length us, event | category | flops | bytes accessed | tf_op | source)
XLA Modules:
  0.0 62.4 jit_solution(4671322933359643297)
XLA Ops:
  1.3 0.0 copy-start
  1.3 60.2 %shard_map.122 = f32[2,8,16,512]{3,2,1,0:T(8,128)S(1)} custom-call(s32[1]{0:T(128)S(6)} %copy.13.cnt_ref, f32[1,8,16,512]{3,2,1,0:T(8,128)} %w_ref.1, bf16[1,8,16,512]{3,2,1,0:T(8,128)(2,1)} %p_ref.1, f32[8,16,512]{2,1,0:T(8,128)} %clon_ref.1, f32[8,16,512]{2,1,0:T(8,128)} %clat_ref.1, f32[64,128]{1,0:T(8,128)} %ov_hbm.1, f32[64,128]{1,0:T(8,128)} %ow_hbm.1, ...), custom_call_target="tpu_custom_call" | custom-call | tf_op jit(solution)/shard_map/pallas_call | solution.py:443
  61.5 0.0 copy-done
  61.5 0.9 %multiply_add_fusion = (f32[1,8,16,512]{3,2,1,0:T(8,128)}, f32[8,16,512]{2,1,0:T(8,128)}) fusion(f32[1,8,16,512]{3,2,1,0:T(8,128)S(1)} %copy-done, f32[2,8,16,512]{3,2,1,0:T(8,128)S(1)} %shard_map.122), kind=kLoop, calls=%fused_computation | loop fusion | flops 196608 | bytes 1310720 | tf_op jit(solution)/shard_map/add | solution.py:471
Async XLA Ops:
  1.3 60.3 %copy-start = (f32[1,8,16,512]{3,2,1,0:T(8,128)S(1)}, f32[1,8,16,512]{3,2,1,0:T(8,128)}, u32[]{:S(2)}) copy-start(f32[1,8,16,512]{3,2,1,0:T(8,128)} %w_ref.1) | copy-start | bytes 786436

commit v5 on v4

--- a/solution.py
+++ b/solution.py
@@ -8,6 +8,7 @@
 from jax.sharding import PartitionSpec as P
 
 SWEEPS = 16
+NAMES = 20
 AROUND = (5, 3, 7, 1, 4, 2, 6)
 VMEM_LIMIT = 24 * 1024 * 1024
 MEM = 32
@@ -52,7 +53,7 @@
     cnt_ref, w_ref, p_ref, clon_ref, clat_ref, ov_hbm, ow_hbm, seg_hbm, kind_hbm, tgt_hbm, op_hbm,
     both_ref,
     wbuf, coef, pbuf, pf, pin, retain, ov_ref, ow_ref, op_ref, seg_ref, kind_ref, tgt_ref,
-    pack, lists, ad, ybuf, s2, zbuf, prod, sibp, half, rsy, sumy, rsz, rs, inc_red, adj_red, fld,
+    pack, lists, names, named_in, ad, ybuf, s2, zbuf, prod, sibp, half, rsy, sumy, rsz, rs, inc_red, adj_red, fld,
     loc_sem, snd, rcv, list_rcv,
 ):
     inc_ref, back_ref = both_ref.at[0], both_ref.at[1]
@@ -121,12 +122,12 @@
     slots = ov_ref.shape[0]
     kinds = op_ref.shape[0]
     live = lax.broadcasted_iota(jnp.int32, (slots, 1), 0) < cnt_ref[0]
-    lane = lax.broadcasted_iota(jnp.int32, (slots, 128), 1)
     for copy in loads[:3]:
         copy.wait()
     target = tgt_ref[...].astype(F32)
-    seg_col = column(seg_ref[...].astype(F32))
-    kind_col = column(kind_ref[...].astype(F32))
+    seg_row = seg_ref[...].astype(F32)
+    kind_row = kind_ref[...].astype(F32)
+    kind_col = column(kind_row)
     named = (
         target == lax.broadcasted_iota(jnp.int32, (TILES, slots), 0).astype(F32)
     ).astype(F32)
@@ -135,7 +136,18 @@
         < lax.broadcasted_iota(jnp.int32, (slots, slots), 1)
     ).astype(F32)
     earlier = jnp.dot(named, upper, preferred_element_type=F32)
-    place = target * 16.0 + jnp.sum(earlier * named, axis=0, keepdims=True)
+    rank = jnp.sum(earlier * named, axis=0, keepdims=True)
+    place = target * 16.0 + rank
+    at_lane = (
+        column(rank) == lax.rem(lax.broadcasted_iota(jnp.int32, (slots, 128), 1), 16).astype(F32)
+    ).astype(F32)
+    told = jnp.dot(
+        jnp.concatenate([named * seg_row, named * kind_row], axis=0), at_lane,
+        precision=HIGHEST, preferred_element_type=F32,
+    )
+    for k in range(TILES):
+        names[k, 0:1] = told[k:k + 1]
+        names[k, 1:2] = told[TILES + k:TILES + k + 1]
     route = (
         lax.broadcasted_iota(jnp.int32, (128, slots), 0).astype(F32) == place
     ).astype(F32)
@@ -148,12 +160,9 @@
         [jnp.where(kind_col == float(k), weighted, 0.0) for k in range(kinds)], axis=1
     )
     pulled = jnp.dot(wide, flat, precision=HIGHEST, preferred_element_type=F32)
-    meta = jnp.where(lane == 0, seg_col, jnp.where(lane == 1, kind_col, 0.0))
-    routed = select(route, split3(jnp.concatenate([pulled, precision, meta], axis=1)))
+    routed = select(route, split3(jnp.concatenate([pulled, precision], axis=1)))
     pack[:, 0:16, :] = routed[:, 0:128].reshape(TILES, 16, 128)
     pack[:, 16:32, :] = routed[:, 128:256].reshape(TILES, 16, 128)
-    routed_meta = routed[:, 256:384].reshape(TILES, 16, 128)
-    pack[:, 32:40, :] = routed_meta[:, 0:8] + pltpu.roll(routed_meta[:, 8:16], 64, 2)
     pf[...] = pin[...].astype(F32)
 
     away = jnp.where((y == 0) & (z < 2), 3, 4)
@@ -170,8 +179,13 @@
             send_sem=snd.at[1], recv_sem=list_rcv.at[d],
             device_id=(m, peer), device_id_type=MESH,
         ).start()
-    own_o = pltpu.make_async_copy(pack.at[t], lists.at[c, t], loc_sem.at[5])
-    own_o.start()
+        remote(names.at[peer], named_in.at[c, t], NAMES, m, peer).start()
+    own_o = [
+        pltpu.make_async_copy(pack.at[t], lists.at[c, t], loc_sem.at[5]),
+        pltpu.make_async_copy(names.at[t], named_in.at[c, t], loc_sem.at[13]),
+    ]
+    for copy in own_o:
+        copy.start()
     for d in AROUND:
         peer = lax.rem(t + d, TILES)
         remote(w_ref.at[0, peer], wbuf.at[t], 2, m, peer).start()
@@ -182,7 +196,8 @@
     for d in (2, 1, 3):
         remote(part, part, 4, lax.rem(y + d, 4) * 8 + z * 2 + c, t).start()
 
-    own_o.wait()
+    for copy in own_o:
+        copy.wait()
     remote(lists.at[c, t], lists.at[c, t], 5, sib, t).start()
     for d in (4, 2, 6, 7, 1, 3, 5):
         source = lax.rem(t + TILES - d, TILES)
@@ -196,15 +211,27 @@
     own_p = pltpu.make_async_copy(pf.at[t], pbuf.at[t], loc_sem.at[4])
     own_p.start()
 
+    got(names.at[pl.ds(0, 7)], NAMES)
+    remote(named_in.at[c], named_in.at[c], NAMES + 1, sib, t).start()
+
     got(lists.at[0], 5)
-
-    rows = lists[...].reshape(2 * TILES, 40, 128)
+    got(named_in.at[0], NAMES + 1)
+
+    rows = lists[...].reshape(2 * TILES, 32, 128)
     pulled_parts = split3(rows[:, 0:16].reshape(256, 128))
     weight_parts = split3(rows[:, 16:32].reshape(256, 128))
-    info = rows[:, 32:40]
-    info = jnp.concatenate([info, pltpu.roll(info, 64, 2)], axis=1).reshape(256, 128)
-    seg_row = as_row(info[:, 0:1])
-    key_row = seg_row + 512.0 * as_row(info[:, 1:2])
+    source = lax.broadcasted_iota(jnp.int32, (TILES, 128), 0)
+    of_source = source == lax.broadcasted_iota(jnp.int32, (TILES, 128), 1) // 16
+
+    def along(which):
+        halves = [
+            jnp.sum(jnp.where(of_source, named_in[core, :, which], 0.0), axis=0, keepdims=True)
+            for core in range(2)
+        ]
+        return jnp.concatenate(halves, axis=1)
+
+    seg_row = along(0)
+    key_row = seg_row + 512.0 * along(1)
     row = lax.broadcasted_iota(jnp.int32, (256, 256), 0)
     fixed = lax.rem(row, 16) * 4 + 2 * c + lax.rem(row // 32, 2)
     for d in (2, 1, 3, 0):
@@ -396,6 +423,8 @@
     left(pf.at[pl.ds(0, 7)], 3)
     left(wbuf.at[pl.ds(0, 6)], 4)
     left(lists.at[0], 5)
+    left(names.at[pl.ds(0, 7)], NAMES)
+    left(named_in.at[0], NAMES + 1)
     left(rows8, 6)
     left(ybuf.at[0], 7)
     left(ybuf.at[1], 17)
@@ -453,7 +482,8 @@
             pltpu.VMEM((1, obs_segment.shape[0]), jnp.int32),
             pltpu.VMEM((1, obs_kind.shape[0]), jnp.int32),
             pltpu.VMEM((1, obs_target.shape[0]), jnp.int32),
-            pltpu.VMEM((TILES, 40, 128), F32), pltpu.VMEM((2, TILES, 40, 128), F32),
+            pltpu.VMEM((TILES, 32, 128), F32), pltpu.VMEM((2, TILES, 32, 128), F32),
+            pltpu.VMEM((TILES, 2, 128), F32), pltpu.VMEM((2, TILES, 2, 128), F32),
             pltpu.VMEM((4, 2, 5, 16, 256), F32), pltpu.VMEM((2, 3, 5, 16, 256), F32),
             pltpu.VMEM((2, 5, 16, 256), F32), pltpu.VMEM((4, 5, 16, 128), F32),
             pltpu.VMEM(block, F32), pltpu.VMEM((TILES, 16, 256), F32),
@@ -462,7 +492,7 @@
             pltpu.VMEM((15, 16, 128), F32),
             pltpu.VMEM((16, 128), F32), pltpu.VMEM((16, 128), F32),
             pltpu.VMEM(block, F32),
-            dma((13,)), dma((20,)), dma((20,)), dma((TILES,)),
+            dma((14,)), dma((22,)), dma((22,)), dma((TILES,)),
         ],
         compiler_params=pltpu.CompilerParams(
             collective_id=0, has_side_effects=True, vmem_limit_bytes=VMEM_LIMIT

time: 62.5 us -> 61.2 us (0.979)
  Pallas kernels: 60.2 us -> 58.9 us
    pallas_call x1, Pallas kernels: 60.2 us -> 58.9 us  [shards(): pl.pallas_call(kernel, out_shape=jax.ShapeDtypeStruct((2,) + block, F32),...]
where the time goes in v5:
time: 61.2 us; the launch traced here: 61.1 us
  Pallas kernels  58.9 us (96%)
  between operations  1.3 us (2%)
  other arithmetic  0.87 us (1%)
    pallas_call x1, Pallas kernels, shards(): pl.pallas_call(kernel, out_shape=jax.ShapeDtypeStruct((2,) + block, F32),...  58.9 us

profile of v5, /device:TPU:1, one launch (start us, length us, event | category | flops | bytes accessed | tf_op | source)
XLA Modules:
  0.0 61.1 jit_solution(4585849935324919138)
XLA Ops:
  1.3 0.0 copy-start
  1.3 58.9 %shard_map.122 = f32[2,8,16,512]{3,2,1,0:T(8,128)S(1)} custom-call(s32[1]{0:T(128)S(6)} %copy.13.cnt_ref, f32[1,8,16,512]{3,2,1,0:T(8,128)} %w_ref.1, bf16[1,8,16,512]{3,2,1,0:T(8,128)(2,1)} %p_ref.1, f32[8,16,512]{2,1,0:T(8,128)} %clon_ref.1, f32[8,16,512]{2,1,0:T(8,128)} %clat_ref.1, f32[64,128]{1,0:T(8,128)} %ov_hbm.1, f32[64,128]{1,0:T(8,128)} %ow_hbm.1, ...), custom_call_target="tpu_custom_call" | custom-call | tf_op jit(solution)/shard_map/pallas_call | solution.py:472
  60.2 0.0 copy-done
  60.2 0.9 %multiply_add_fusion = (f32[1,8,16,512]{3,2,1,0:T(8,128)}, f32[8,16,512]{2,1,0:T(8,128)}) fusion(f32[1,8,16,512]{3,2,1,0:T(8,128)S(1)} %copy-done, f32[2,8,16,512]{3,2,1,0:T(8,128)S(1)} %shard_map.122), kind=kLoop, calls=%fused_computation | loop fusion | flops 196608 | bytes 1310720 | tf_op jit(solution)/shard_map/add | solution.py:501
Async XLA Ops:
  1.3 59.0 %copy-start = (f32[1,8,16,512]{3,2,1,0:T(8,128)S(1)}, f32[1,8,16,512]{3,2,1,0:T(8,128)}, u32[]{:S(2)}) copy-start(f32[1,8,16,512]{3,2,1,0:T(8,128)} %w_ref.1) | copy-start | bytes 786436

commit v6 on v5

--- a/solution.py
+++ b/solution.py
@@ -9,7 +9,7 @@
 
 SWEEPS = 16
 NAMES = 20
-AROUND = (5, 3, 7, 1, 4, 2, 6)
+AROUND = (5, 3, 1, 7, 4, 2, 6)
 VMEM_LIMIT = 24 * 1024 * 1024
 MEM = 32
 TILES = 8
@@ -288,7 +288,7 @@
             here, down_before, up = after, down, up_after
         return carry
 
-    lax.fori_loop(0, SWEEPS, sweep, 0, unroll=4)
+    lax.fori_loop(0, SWEEPS, sweep, 0, unroll=8)
     def pass_on(near, sem):
         got(ybuf.at[near], sem)
         s2[near] = ad[0, near] + ybuf[near, 0] + ybuf[near, 1] + ybuf[near, 2]
@@ -397,7 +397,7 @@
             here, flux, down_before, up = after, flux_after, down, up_after
         return carry
 
-    lax.fori_loop(0, SWEEPS, sweep_back, 0, unroll=4)
+    lax.fori_loop(0, SWEEPS, sweep_back, 0, unroll=8)
     for d in AROUND:
         peer = lax.rem(t + d, TILES)
         remote(prod.at[peer], back_ref.at[t], 15, m, peer).start()

time: 61.2 us -> 60.1 us (0.982)
  the two profiles are of different devices: /device:TPU:1 before, /device:TPU:33 now
where the time goes in v6:
time: 60.1 us; the launch traced here: 60 us
  Pallas kernels  57.9 us (96%)
  between operations  1.3 us (2%)
  other arithmetic  0.87 us (1%)
    pallas_call x1, Pallas kernels, shards(): pl.pallas_call(kernel, out_shape=jax.ShapeDtypeStruct((2,) + block, F32),...  57.9 us

profile of v6, /device:TPU:33, one launch (start us, length us, event | category | flops | bytes accessed | tf_op | source)
XLA Modules:
  0.0 60.0 jit_solution(8352600008658056777)
XLA Ops:
  1.3 0.0 copy-start
  1.3 57.9 %shard_map.122 = f32[2,8,16,512]{3,2,1,0:T(8,128)S(1)} custom-call(s32[1]{0:T(128)S(6)} %copy.13.cnt_ref, f32[1,8,16,512]{3,2,1,0:T(8,128)} %w_ref.1, bf16[1,8,16,512]{3,2,1,0:T(8,128)(2,1)} %p_ref.1, f32[8,16,512]{2,1,0:T(8,128)} %clon_ref.1, f32[8,16,512]{2,1,0:T(8,128)} %clat_ref.1, f32[64,128]{1,0:T(8,128)} %ov_hbm.1, f32[64,128]{1,0:T(8,128)} %ow_hbm.1, ...), custom_call_target="tpu_custom_call" | custom-call | tf_op jit(solution)/shard_map/pallas_call | solution.py:472
  59.2 0.0 copy-done
  59.2 0.9 %multiply_add_fusion = (f32[1,8,16,512]{3,2,1,0:T(8,128)}, f32[8,16,512]{2,1,0:T(8,128)}) fusion(f32[1,8,16,512]{3,2,1,0:T(8,128)S(1)} %copy-done, f32[2,8,16,512]{3,2,1,0:T(8,128)S(1)} %shard_map.122), kind=kLoop, calls=%fused_computation | loop fusion | flops 196608 | bytes 1310720 | tf_op jit(solution)/shard_map/add | solution.py:501
Async XLA Ops:
  1.3 57.9 %copy-start = (f32[1,8,16,512]{3,2,1,0:T(8,128)S(1)}, f32[1,8,16,512]{3,2,1,0:T(8,128)}, u32[]{:S(2)}) copy-start(f32[1,8,16,512]{3,2,1,0:T(8,128)} %w_ref.1) | copy-start | bytes 786436

commit v7 on v6

--- a/solution.py
+++ b/solution.py
@@ -288,7 +288,7 @@
             here, down_before, up = after, down, up_after
         return carry
 
-    lax.fori_loop(0, SWEEPS, sweep, 0, unroll=8)
+    lax.fori_loop(0, SWEEPS, sweep, 0, unroll=16)
     def pass_on(near, sem):
         got(ybuf.at[near], sem)
         s2[near] = ad[0, near] + ybuf[near, 0] + ybuf[near, 1] + ybuf[near, 2]
@@ -397,7 +397,7 @@
             here, flux, down_before, up = after, flux_after, down, up_after
         return carry
 
-    lax.fori_loop(0, SWEEPS, sweep_back, 0, unroll=8)
+    lax.fori_loop(0, SWEEPS, sweep_back, 0, unroll=16)
     for d in AROUND:
         peer = lax.rem(t + d, TILES)
         remote(prod.at[peer], back_ref.at[t], 15, m, peer).start()

time: 60.1 us -> 60 us (level)
  no operation moved by 1% of the time
where the time goes in v7:
time: 60 us; the launch traced here: 59.9 us
  Pallas kernels  57.8 us (96%)
  between operations  1.3 us (2%)
  other arithmetic  0.87 us (1%)
    pallas_call x1, Pallas kernels, shards(): pl.pallas_call(kernel, out_shape=jax.ShapeDtypeStruct((2,) + block, F32),...  57.8 us

profile of v7, /device:TPU:33, one launch (start us, length us, event | category | flops | bytes accessed | tf_op | source)
XLA Modules:
  0.0 59.9 jit_solution(2973648296517540953)
XLA Ops:
  1.3 0.0 copy-start
  1.3 57.8 %shard_map.122 = f32[2,8,16,512]{3,2,1,0:T(8,128)S(1)} custom-call(s32[1]{0:T(128)S(6)} %copy.13.cnt_ref, f32[1,8,16,512]{3,2,1,0:T(8,128)} %w_ref.1, bf16[1,8,16,512]{3,2,1,0:T(8,128)(2,1)} %p_ref.1, f32[8,16,512]{2,1,0:T(8,128)} %clon_ref.1, f32[8,16,512]{2,1,0:T(8,128)} %clat_ref.1, f32[64,128]{1,0:T(8,128)} %ov_hbm.1, f32[64,128]{1,0:T(8,128)} %ow_hbm.1, ...), custom_call_target="tpu_custom_call" | custom-call | tf_op jit(solution)/shard_map/pallas_call | solution.py:472
  59.1 0.0 copy-done
  59.1 0.9 %multiply_add_fusion = (f32[1,8,16,512]{3,2,1,0:T(8,128)}, f32[8,16,512]{2,1,0:T(8,128)}) fusion(f32[1,8,16,512]{3,2,1,0:T(8,128)S(1)} %copy-done, f32[2,8,16,512]{3,2,1,0:T(8,128)S(1)} %shard_map.122), kind=kLoop, calls=%fused_computation | loop fusion | flops 196608 | bytes 1310720 | tf_op jit(solution)/shard_map/add | solution.py:501
Async XLA Ops:
  1.3 57.8 %copy-start = (f32[1,8,16,512]{3,2,1,0:T(8,128)S(1)}, f32[1,8,16,512]{3,2,1,0:T(8,128)}, u32[]{:S(2)}) copy-start(f32[1,8,16,512]{3,2,1,0:T(8,128)} %w_ref.1) | copy-start | bytes 786436
